TPU v7x, 32 devices: a whole 2x2x4 slice. The times are simulated.
32 devices in a mesh: dp: 4 (over z), expert: 8 (over y, x, core).
Axes of the slice: x: 2, y: 2, z: 4, core: 2. Of those that a mesh axis runs over, the one named last changes fastest.
Arguments:
- tokens: bfloat16 [32768, 768], P(('dp', 'expert')), may hold values from -6 to 6
- lengths: int32 [32], P(('dp', 'expert')), may hold values from 128 to 1024, as said below
- expert_index: int32 [32768], P(('dp', 'expert')), may hold values from 0 to 7, as said below
- centroids: float32 [8, 768], replicated, may hold values from -0.15625 to 0.15625
- input_weight: bfloat16 [768, 2304], replicated, may hold values from -0.3125 to 0.3125
- output_weight: bfloat16 [768, 768], replicated, may hold values from -0.875 to 0.875
- first_gain: float32 [768], replicated, may hold values from 0.5 to 1.5
- first_shift: float32 [768], replicated, may hold values from -1 to 1
- second_gain: float32 [768], replicated, may hold values from 0.5 to 1.5
- second_shift: float32 [768], replicated, may hold values from -1 to 1
- up_weight: bfloat16 [8, 768, 3072], P('expert'), may hold values from -0.21875 to 0.21875
- down_weight: bfloat16 [8, 3072, 768], P('expert'), may hold values from -0.3125 to 0.3125
- cotangent: bfloat16 [32768, 768], P(('dp', 'expert')), may hold values from -6 to 6
Outputs:
- layer_output: bfloat16 [32768, 768], P(('dp', 'expert'))
- input_gradient: bfloat16 [32768, 768], P(('dp', 'expert'))
- input_weight_gradient: float32 [768, 2304], P('dp')
- output_weight_gradient: float32 [768, 768], P('dp')
- first_gain_gradient: float32 [768], P('dp')
- first_shift_gradient: float32 [768], P('dp')
- second_gain_gradient: float32 [768], P('dp')
- second_shift_gradient: float32 [768], P('dp')
- up_weight_gradient: float32 [8, 768, 3072], P('expert', 'dp')
- down_weight_gradient: float32 [8, 3072, 768], P('expert', 'dp')
Inputs may be any that keep to these rules, and one draw needn't show every extreme that they name: `lengths`: some sequence has exactly 1024 live positions. `expert_index`: in each aligned block of 1024 rows (the sequences of one device), at most 128 rows inside their sequence's length name any one expert, and one expert, the same in every block, is named by exactly 128 of them.
All inputs are finite; a program needn't handle non-finite values.
Results may differ from a plain program's by a relative error of at most 0.015.
Values may be sent and summed in bfloat16 or wider, within the bound.
No kernel may reach another device: no remote copies, remote signals or barrier semaphores. Data moves between devices by JAX's collectives and lax.ppermute only.
A program may use at most 256 MiB of HBM per device.

v0:
```python
import jax
import jax.numpy as jnp
from jax import lax
from jax.sharding import PartitionSpec as P

HEADS = 12
LEN = 1024


epsilon = 1e-05
excluded = -1e30


def layer_norm(values, norm_gain, norm_shift):
    average = jnp.mean(values, axis=-1, keepdims=True)
    centred = values - average
    variance = jnp.mean(centred * centred, axis=-1, keepdims=True)
    return centred * lax.rsqrt(variance + epsilon) * norm_gain + norm_shift


def exact_gelu(values):
    return jax.nn.gelu(values, approximate=False)


def masked_scores(query_block, key_rows, lengths, first_row, scale_factor):
    scores = (
        jnp.einsum("sqhd,skhd->shqk", query_block, key_rows, preferred_element_type=jnp.float32)
        * scale_factor
    )
    rows = first_row + jnp.arange(query_block.shape[1])
    columns = jnp.arange(key_rows.shape[1])
    causal = columns[None, :] <= rows[:, None]
    inside = columns[None, :] < lengths[:, None]
    allowed = causal[None, None, :, :] & inside[:, None, None, :]
    return jnp.where(allowed, scores, excluded)


def on_device(
    tokens,
    lengths,
    expert_index,
    centroids,
    input_weight,
    output_weight,
    first_gain,
    first_shift,
    second_gain,
    second_shift,
    up_weight,
    down_weight,
    cotangent,
):
    row_count = tokens.shape[0]
    width = tokens.shape[1]
    sequences = lengths.shape[0]
    experts = centroids.shape[0]
    capacity = row_count // experts
    head_size = width // HEADS
    block = min(512, LEN)
    scale_factor = head_size ** (-0.5)
    split_heads = (sequences, LEN, HEADS, head_size)
    positions = jnp.arange(row_count)
    present = positions % LEN < jnp.repeat(lengths, LEN)
    row_mask = present.astype(jnp.float32)[:, None]
    inputs_float = tokens.astype(jnp.float32)
    normed, first_back = jax.vjp(layer_norm, inputs_float, first_gain, first_shift)
    normed_low = normed.astype(jnp.bfloat16)
    projected = jnp.dot(normed_low, input_weight, preferred_element_type=jnp.float32)
    queries = projected[:, :width].astype(jnp.bfloat16).reshape(split_heads)
    keys = projected[:, width : 2 * width].astype(jnp.bfloat16).reshape(split_heads)
    values = projected[:, 2 * width :].astype(jnp.bfloat16).reshape(split_heads)
    mixed_blocks = []
    kept_top = []
    kept_total = []
    for first_row in range(0, LEN, block):
        upto = first_row + block
        scores = masked_scores(
            queries[:, first_row:upto], keys[:, :upto], lengths, first_row, scale_factor
        )
        top = jnp.max(scores, axis=-1, keepdims=True)
        weights = jnp.exp(scores - top)
        total = jnp.sum(weights, axis=-1, keepdims=True)
        probs_low = (weights / total).astype(jnp.bfloat16)
        mixed_blocks.append(
            jnp.einsum(
                "shqk,skhd->sqhd", probs_low, values[:, :upto], preferred_element_type=jnp.float32
            )
        )
        kept_top.append(top)
        kept_total.append(total)
    mixed_low = jnp.concatenate(mixed_blocks, axis=1).reshape(row_count, width).astype(jnp.bfloat16)
    branch = jnp.dot(mixed_low, output_weight, preferred_element_type=jnp.float32)
    residual = inputs_float + row_mask * branch
    hidden, second_back = jax.vjp(layer_norm, residual, second_gain, second_shift)
    hidden_low = hidden.astype(jnp.bfloat16)
    onehot = expert_index[:, None] == jnp.arange(experts)[None, :]
    picked = jnp.dot(
        onehot.astype(jnp.float32),
        centroids,
        precision=lax.Precision.HIGHEST,
        preferred_element_type=jnp.float32,
    )
    gate = jax.nn.sigmoid(jnp.sum(hidden * picked, axis=-1))
    routed = onehot & present[:, None]
    counts = jnp.cumsum(routed.astype(jnp.int32), axis=0)
    slot = jnp.sum(jnp.where(routed, counts - 1, 0), axis=1)
    target = jnp.where(present, expert_index * capacity + slot, experts * capacity)
    outgoing = (
        jnp.zeros((experts * capacity, width), jnp.bfloat16)
        .at[target]
        .set(hidden_low, mode="drop")
        .reshape(experts, capacity, width)
    )
    arrived = lax.all_to_all(outgoing, "expert", split_axis=0, concat_axis=0, tiled=True)
    count = arrived.shape[1]
    flat = arrived.reshape(-1, width)
    upper = jnp.dot(flat, up_weight[0], preferred_element_type=jnp.float32)
    expert_active = exact_gelu(upper).astype(jnp.bfloat16)
    produced = jnp.dot(expert_active, down_weight[0], preferred_element_type=jnp.float32).astype(
        jnp.bfloat16
    )
    returned = lax.all_to_all(
        produced.reshape(experts, count, width), "expert", split_axis=0, concat_axis=0, tiled=True
    )
    results = (returned, arrived)
    returned = results[0]
    arrived = results[1]
    expert_term = jnp.take(
        returned.reshape(experts * capacity, width), target, axis=0, mode="fill", fill_value=0
    ).astype(jnp.float32)
    scaled = row_mask * gate[:, None]
    layer_output = (residual + scaled * expert_term).astype(jnp.bfloat16)
    upstream = cotangent.astype(jnp.float32)
    produced_gradient = (scaled * upstream).astype(jnp.bfloat16)
    logit_gradient = row_mask[:, 0] * jnp.sum(upstream * expert_term, axis=-1) * gate * (1.0 - gate)
    gradient_outgoing = (
        jnp.zeros((experts * capacity, width), jnp.bfloat16)
        .at[target]
        .set(produced_gradient, mode="drop")
        .reshape(experts, capacity, width)
    )
    arrived_gradient = lax.all_to_all(
        gradient_outgoing, "expert", split_axis=0, concat_axis=0, tiled=True
    ).reshape(-1, width)
    arrived_rows = arrived.reshape(-1, width)
    upper = jnp.dot(arrived_rows, up_weight[0], preferred_element_type=jnp.float32)
    active_float, gelu_back = jax.vjp(exact_gelu, upper)
    active = active_float.astype(jnp.bfloat16)
    dp_count = lax.axis_size("dp")
    part = active
    down_weight_gradient = lax.psum_scatter(
        jnp.einsum("rf,rd->fd", part, arrived_gradient, preferred_element_type=jnp.float32).astype(
            jnp.bfloat16
        ),
        "dp",
        scatter_dimension=0,
        tiled=True,
    ).astype(jnp.float32)
    active_gradient = jnp.einsum(
        "rd,fd->rf", arrived_gradient, down_weight[0], preferred_element_type=jnp.float32
    )
    upper_gradient = gelu_back(active_gradient)[0].astype(jnp.bfloat16)
    part = arrived_rows
    up_weight_gradient = lax.psum_scatter(
        jnp.einsum("rd,rf->df", part, upper_gradient, preferred_element_type=jnp.float32).astype(
            jnp.bfloat16
        ),
        "dp",
        scatter_dimension=0,
        tiled=True,
    ).astype(jnp.float32)
    sent_back = jnp.einsum(
        "rf,df->rd", upper_gradient, up_weight[0], preferred_element_type=jnp.float32
    ).astype(jnp.bfloat16)
    hidden_back = lax.all_to_all(
        sent_back.reshape(experts, capacity, width),
        "expert",
        split_axis=0,
        concat_axis=0,
        tiled=True,
    )
    expert_hidden = jnp.take(
        hidden_back.reshape(experts * capacity, width), target, axis=0, mode="fill", fill_value=0
    ).astype(jnp.float32)
    hidden_gradient = expert_hidden + logit_gradient[:, None] * picked
    residual_part, second_gain_gradient, second_shift_gradient = second_back(hidden_gradient)
    residual_gradient = upstream + residual_part
    branch_gradient = (row_mask * residual_gradient).astype(jnp.bfloat16)
    output_weight_gradient = jnp.einsum(
        "rd,re->de", mixed_low, branch_gradient, preferred_element_type=jnp.float32
    )
    mixed_gradient = (
        jnp.einsum("re,de->rd", branch_gradient, output_weight, preferred_element_type=jnp.float32)
        .astype(jnp.bfloat16)
        .reshape(split_heads)
    )
    query_blocks = []
    key_gradient = jnp.zeros(split_heads, jnp.float32)
    value_gradient = jnp.zeros(split_heads, jnp.float32)
    for number, first_row in enumerate(range(0, LEN, block)):
        upto = first_row + block
        query_block = queries[:, first_row:upto]
        scores = masked_scores(query_block, keys[:, :upto], lengths, first_row, scale_factor)
        probs = jnp.exp(scores - kept_top[number]) / kept_total[number]
        probs_low = probs.astype(jnp.bfloat16)
        incoming = mixed_gradient[:, first_row:upto]
        prob_gradient = jnp.einsum(
            "sqhd,skhd->shqk", incoming, values[:, :upto], preferred_element_type=jnp.float32
        )
        inner = jnp.sum(probs * prob_gradient, axis=-1, keepdims=True)
        score_gradient = (probs * (prob_gradient - inner)).astype(jnp.bfloat16)
        query_blocks.append(
            jnp.einsum(
                "shqk,skhd->sqhd",
                score_gradient,
                keys[:, :upto],
                preferred_element_type=jnp.float32,
            )
            * scale_factor
        )
        key_gradient = key_gradient.at[:, :upto].add(
            jnp.einsum(
                "shqk,sqhd->skhd", score_gradient, query_block, preferred_element_type=jnp.float32
            )
            * scale_factor
        )
        value_gradient = value_gradient.at[:, :upto].add(
            jnp.einsum("shqk,sqhd->skhd", probs_low, incoming, preferred_element_type=jnp.float32)
        )
    query_gradient = jnp.concatenate(query_blocks, axis=1)
    projected_gradient = jnp.concatenate(
        [
            query_gradient.reshape(row_count, width),
            key_gradient.reshape(row_count, width),
            value_gradient.reshape(row_count, width),
        ],
        axis=1,
    ).astype(jnp.bfloat16)
    input_weight_gradient = jnp.einsum(
        "rd,re->de", normed_low, projected_gradient, preferred_element_type=jnp.float32
    )
    normed_gradient = jnp.einsum(
        "re,de->rd", projected_gradient, input_weight, preferred_element_type=jnp.float32
    )
    input_part, first_gain_gradient, first_shift_gradient = first_back(normed_gradient)
    input_gradient = (residual_gradient + input_part).astype(jnp.bfloat16)
    gain_columns = jnp.stack(
        [first_gain_gradient, first_shift_gradient, second_gain_gradient, second_shift_gradient],
        axis=1,
    )
    total_input, total_output, total_gains = lax.psum(
        (input_weight_gradient, output_weight_gradient, gain_columns), ("dp", "expert")
    )
    share = width // dp_count
    begin = lax.axis_index("dp") * share
    input_share = lax.dynamic_slice_in_dim(total_input, begin, share, 0)
    output_share = lax.dynamic_slice_in_dim(total_output, begin, share, 0)
    gain_share = lax.dynamic_slice_in_dim(total_gains, begin, share, 0)
    return (
        layer_output,
        input_gradient,
        input_share,
        output_share,
        gain_share[:, 0],
        gain_share[:, 1],
        gain_share[:, 2],
        gain_share[:, 3],
        up_weight_gradient[None],
        down_weight_gradient[None],
    )


def solution(mesh):
    return jax.shard_map(
        on_device,
        mesh=mesh,
        in_specs=(
            P(("dp", "expert"), None),
            P(("dp", "expert")),
            P(("dp", "expert")),
            P(),
            P(),
            P(),
            P(),
            P(),
            P(),
            P(),
            P("expert", None, None),
            P("expert", None, None),
            P(("dp", "expert"), None),
        ),
        out_specs=(
            P(("dp", "expert"), None),
            P(("dp", "expert"), None),
            P("dp", None),
            P("dp", None),
            P("dp"),
            P("dp"),
            P("dp"),
            P("dp"),
            P("expert", "dp", None),
            P("expert", "dp", None),
        ),
        check_vma=False,
    )
```

profile of v0, /device:TPU:0, one launch (start us, length us, event | category | flops | bytes accessed | tf_op | source)
XLA Modules:
  0.0 812.6 jit_solution(16364089621944587762)
XLA Ops:
  11.3 5.1 reduce-window.6
  20.4 2.6 copy.43
  23.1 1.8 convert_reduce_fusion
  24.9 1.9 fusion.38
  27.4 4.4 convolution_convert_fusion
  31.8 2.3 fusion.118
  34.1 2.6 copy.45
  36.6 2.6 copy.46
  39.2 3.0 copy.44
  43.5 13.4 %fusion.85 = f32[12,512,1024]{2,1,0:T(8,128)} fusion(bf16[1024,12,64]{0,2,1:T(8,128)(2,1)} %bitcast.177, bf16[1,1024,12,64]{1,3,2,0:T(8,128)(2,1)} %bitcast.181), kind=kOutput, calls=%fused_computation.133 | convolution fusion | flops 805306368 | bytes 27525120 | tf_op jit(solution)/shard_map/sqhd,skhd->shqk/dot_general | solution.py:27
  56.9 11.1 %fusion.121 = (f32[12,512]{1,0:T(8,128)}, f32[12,512,512]{1,2,0:T(8,128)}) fusion(pred[512,512]{0,1:T(8,128)(4,1)} %fusion.79, bf16[1,1024,12,64]{1,3,2,0:T(8,128)(2,1)} %bitcast.182, bf16[1,1024,12,64]{1,3,2,0:T(8,128)(2,1)} %bitcast.178), kind=kOutput, calls=%fused_computation.196 | convolution fusion | flops 415236608 | bytes 14442496 | tf_op jit(solution)/shard_map/sub | solution.py:81
  68.0 34.4 %fusion.120 = (f32[12,512]{1,0:T(8,128)}, f32[12,512,1024]{2,1,0:T(8,128)}) fusion(f32[12,512,1024]{2,1,0:T(8,128)} %fusion.85, pred[512,1024]{1,0:T(8,128)(4,1)} %fusion.49), kind=kOutput, calls=%fused_computation.195 | output fusion | flops 37749760 | bytes 50880512 | tf_op jit(solution)/shard_map/sub | solution.py:81
  102.3 6.0 fusion.74
  108.4 10.3 %fusion.71 = bf16[1,512,12,64]{1,3,2,0:T(8,128)(2,1)S(1)} fusion(bf16[1024,12,64]{0,2,1:T(8,128)(2,1)S(1)} %bitcast.195, f32[12,512,1024]{2,1,0:T(8,128)} %get-tuple-element.121, f32[12,512]{1,0:T(8,128)S(1)} %copy-done.50), kind=kOutput, calls=%fused_computation.114 | convolution fusion | flops 818282496 | bytes 27549696 | tf_op jit(solution)/shard_map/shqk,skhd->sqhd/dot_general | solution.py:85
  119.0 1.7 copy-done.2
  123.6 4.8 fusion.48
  128.5 2.6 copy.50
  132.4 7.0 scatter_custom_fusion
  139.4 26.6 %all_to_all.20 = bf16[8,128,768]{2,1,0:T(8,128)(2,1)S(1)} all-to-all(bf16[8,128,768]{2,1,0:T(8,128)(2,1)} %bitcast.188), channel_id=1, replica_groups=mesh['dp'=4,'expert'=8] {'expert'}, dimensions={0} | all-to-all | bytes 3145728 | tf_op jit(solution)/shard_map/all_to_all | solution.py:114
  166.0 35.7 %multiply_convert_fusion.2 = (bf16[1024,3072]{1,0:T(8,128)(2,1)S(1)}, f32[1024,3072]{1,0:T(8,128)}, f32[1024,3072]{1,0:T(8,128)}) fusion(bf16[1024,768]{1,0:T(8,128)(2,1)S(1)} %bitcast.191, bf16[1,768,3072]{2,1,0:T(8,128)(2,1)} %param.37), kind=kOutput, calls=%fused_computation.16 | convolution fusion | flops 5036310528 | bytes 37748736 | tf_op jit(solution)/shard_map/dot_general | solution.py:117
  201.7 10.7 %fusion.57 = bf16[1024,768]{1,0:T(8,128)(2,1)} fusion(bf16[1024,3072]{1,0:T(8,128)(2,1)S(1)} %get-tuple-element.106, bf16[1,3072,768]{2,1,0:T(8,128)(2,1)} %param.38), kind=kOutput, calls=%fused_computation.102 | convolution fusion | flops 4832624640 | bytes 12582912 | tf_op jit(solution)/shard_map/dot_general | solution.py:119
  212.4 4.3 all-to-all-start.1
  216.7 2.6 copy.52
  219.3 18.4 %all-to-all-done.1 = bf16[8,128,768]{2,1,0:T(8,128)(2,1)} async-done(((bf16[8,128,768]{2,1,0:T(8,128)(2,1)}), bf16[8,128,768]{2,1,0:T(8,128)(2,1)}, u32[]{:S(2)}, u32[]{:S(2)}) %all-to-all-start.1) | async-done | bytes 1572896 | tf_op jit(solution)/shard_map/all_to_all | solution.py:122
  237.7 7.2 gather_fusion
  244.9 2.6 copy.51
  247.5 4.4 fusion.40
  251.9 2.6 copy.53
  254.5 7.0 scatter_custom_fusion.1
  261.5 24.7 %all_to_all.21 = bf16[8,128,768]{2,1,0:T(8,128)(2,1)S(1)} all-to-all(bf16[8,128,768]{2,1,0:T(8,128)(2,1)} %bitcast.187), channel_id=1, replica_groups=mesh['dp'=4,'expert'=8] {'expert'}, dimensions={0} | all-to-all | bytes 3145728 | tf_op jit(solution)/shard_map/all_to_all | solution.py:142
  286.2 16.4 %add_convert_fusion = bf16[1024,3072]{1,0:T(8,128)(2,1)} fusion(f32[1024,3072]{1,0:T(8,128)} %get-tuple-element.107, f32[1024,3072]{1,0:T(8,128)} %get-tuple-element.127, bf16[1024,768]{1,0:T(8,128)(2,1)S(1)} %bitcast.199, bf16[1,3072,768]{2,1,0:T(8,128)(2,1)} %param.38), kind=kOutput, calls=%fused_computation.15 | convolution fusion | flops 4875878400 | bytes 37748736 | tf_op jit(solution)/shard_map/rd,fd->rf/dot_general | solution.py:159
  302.6 9.5 %fusion.54 = bf16[1024,768]{1,0:T(8,128)(2,1)} fusion(bf16[1024,3072]{1,0:T(8,128)(2,1)} %add_convert_fusion, bf16[1,768,3072]{2,1,0:T(8,128)(2,1)} %param.37), kind=kOutput, calls=%fused_computation.101 | convolution fusion | flops 4832624640 | bytes 12582912 | tf_op jit(solution)/shard_map/rf,df->rd/dot_general | solution.py:172
  312.1 4.4 all-to-all-start.3
  316.6 21.0 %all-to-all-done.3 = bf16[8,128,768]{2,1,0:T(8,128)(2,1)} async-done(((bf16[8,128,768]{2,1,0:T(8,128)(2,1)}), bf16[8,128,768]{2,1,0:T(8,128)(2,1)}, u32[]{:S(2)}, u32[]{:S(2)}) %all-to-all-start.3) | async-done | bytes 1572896 | tf_op jit(solution)/shard_map/all_to_all | solution.py:175
  337.5 7.2 gather_fusion.1
  344.7 2.6 copy.54
  347.4 5.5 multiply_reduce_fusion.2
  353.0 4.2 fusion.116
  359.8 2.8 fusion.124
  365.1 3.2 fusion.60
  368.3 5.7 multiply_reduce_fusion.1
  374.0 6.9 multiply_convert_fusion.1
  380.9 2.0 fusion.78
  382.9 3.2 multiply_bitcast_fusion
  386.1 17.8 %multiply_reduce_fusion = (f32[12,512]{1,0:T(8,128)}, f32[12,512,1024]{2,1,0:T(8,128)}) fusion(f32[12,512,1024]{2,1,0:T(8,128)} %get-tuple-element.121, f32[12,512]{1,0:T(8,128)} %get-tuple-element.120, bf16[1024,12,64]{0,2,1:T(8,128)(2,1)} %bitcast.194, bf16[1,1024,12,64]{1,3,2,0:T(8,128)(2,1)} %bitcast.215), kind=kOutput, calls=%fused_computation.7 | convolution fusion | flops 824174592 | bytes 52748288 | tf_op jit(solution)/shard_map/sqhd,skhd->shqk/dot_general | solution.py:207
  403.9 10.6 %fusion.42 = bf16[1,1024,12,64]{1,3,2,0:T(8,128)(2,1)S(1)} fusion(f32[1,512,12,64]{1,3,2,0:T(8,128)} %fusion.60, bf16[1,1024,12,64]{1,3,2,0:T(8,128)(2,1)} %bitcast.216, f32[12,512,1024]{2,1,0:T(8,128)} %get-tuple-element.121, f32[12,512]{1,0:T(8,128)} %get-tuple-element.120), kind=kOutput, calls=%fused_computation.81 | convolution fusion | flops 819462144 | bytes 29130752 | tf_op jit(solution)/shard_map/shqk,sqhd->skhd/dot_general | solution.py:228
  414.5 21.8 %multiply_convert_fusion = bf16[12,512,1024]{2,1,0:T(8,128)(2,1)} fusion(f32[12,512,1024]{2,1,0:T(8,128)} %get-tuple-element.131, f32[12,512]{1,0:T(8,128)S(1)} %copy-done.52, f32[12,512,1024]{2,1,0:T(8,128)} %get-tuple-element.121, f32[12,512]{1,0:T(8,128)S(1)} %copy-done.51), kind=kLoop, calls=%fused_computation.6 | loop fusion | flops 25165824 | bytes 62963712 | tf_op jit(solution)/shard_map/convert_element_type | solution.py:211
  436.4 8.6 %fusion.77 = bf16[1,512,12,64]{1,3,2,0:T(8,128)(2,1)S(1)} fusion(bf16[1024,12,64]{0,2,1:T(8,128)(2,1)S(1)} %bitcast.180, bf16[12,512,1024]{2,1,0:T(8,128)(2,1)} %multiply_convert_fusion), kind=kOutput, calls=%fused_computation.116 | convolution fusion | flops 806092800 | bytes 14942208 | tf_op jit(solution)/shard_map/shqk,skhd->sqhd/dot_general | solution.py:213
  445.1 6.9 fusion.43
  454.6 7.1 fusion.50
  461.7 9.1 %convolution_convert_fusion.1 = bf16[3072,768]{1,0:T(8,128)(2,1)} fusion(bf16[1024,3072]{1,0:T(8,128)(2,1)} %copy-done.72, bf16[1024,768]{1,0:T(8,128)(2,1)} %bitcast.200), kind=kOutput, calls=%fused_computation.46 | convolution fusion | flops 4834197504 | bytes 12582912 | tf_op jit(solution)/shard_map/rf,rd->fd/dot_general | solution.py:152
  470.9 9.5 %convolution_convert_fusion.2 = bf16[768,3072]{1,0:T(8,128)(2,1)} fusion(bf16[1024,768]{1,0:T(8,128)(2,1)} %bitcast.192, bf16[1024,3072]{1,0:T(8,128)(2,1)} %add_convert_fusion), kind=kOutput, calls=%fused_computation.47 | convolution fusion | flops 4834197504 | bytes 12582912 | tf_op jit(solution)/shard_map/rd,rf->df/dot_general | solution.py:165
  482.3 2.6 copy.60
  484.9 7.9 fusion.123
  493.4 3.7 copy.58
  497.1 3.0 fusion.39
  502.9 2.7 add_convert_fusion.1
  505.6 2.6 copy.61
  508.9 43.2 %psum.23 = f32[768,4]{0,1:T(4,128)} all-reduce(f32[768,4]{0,1:T(4,128)S(1)} %pad_maximum_fusion.5), channel_id=1, replica_groups=mesh['dp'=4,'expert'=8] {'dp','expert'}, use_global_device_ids=true, to_apply=%region_27.29 | all-reduce | flops 3072 | bytes 24576 | tf_op jit(solution)/shard_map/psum | solution.py:251
  553.6 240.9 %all-reduce.5.cloned.1.call-done = (f32[768,2304]{1,0:T(8,128)}, f32[768,768]{1,0:T(8,128)}) async-done(((f32[768,2304]{1,0:T(8,128)}, f32[768,768]{1,0:T(8,128)}), (f32[768,2304]{1,0:T(8,128)}, f32[768,768]{1,0:T(8,128)})) %all-reduce.5.cloned.1.call-update) | async-done | bytes 9437200 | tf_op jit(solution)/shard_map/psum | solution.py:251
  794.5 1.9 constant_dynamic-slice_fusion.1
  796.4 2.8 constant_dynamic-slice_fusion.2
  799.2 2.8 bitcast_convert_fusion
  802.1 2.9 bitcast_convert_fusion.1
  (197 shorter events, 27.9 us)
Async XLA Ops:
  8.0 19.3 %copy-start = (bf16[768,2304]{1,0:T(8,128)(2,1)S(1)}, bf16[768,2304]{1,0:T(8,128)(2,1)}, u32[]{:S(2)}) copy-start(bf16[768,2304]{1,0:T(8,128)(2,1)} %param.31) | copy-start | bytes 10616836
  9.9 109.0 %copy-start.56 = (f32[1024]{0:T(1024)}, f32[1024]{0:T(1024)S(1)}, u32[]{:S(2)}) copy-start(f32[1024]{0:T(1024)S(1)} %fusion.106) | copy-start | bytes 12292
  20.4 6.9 copy-start.46
  20.4 6.9 copy-start.68
  23.1 4.3 copy-start.1
  24.9 6.9 copy-start.30
  27.4 4.4 copy-start.37
  36.6 5.6 copy-start.64
  102.3 6.1 copy-start.22
  102.3 6.1 copy-start.50
  119.0 3.8 copy-start.24
  122.7 5.7 copy-start.5
  122.8 5.7 copy-start.28
  123.2 5.3 copy-start.43
  123.6 4.9 copy-start.32
  128.5 2.6 copy-start.65
  132.4 69.2 %copy-start.58 = (s32[1024]{0:T(1024)}, s32[1024]{0:T(1024)S(1)}, u32[]{:S(2)}) copy-start(s32[1024]{0:T(1024)S(1)} %get-tuple-element.105) | copy-start | bytes 12292
  166.0 35.7 %copy-start.21 = (bf16[8,128,768]{2,1,0:T(8,128)(2,1)}, bf16[8,128,768]{2,1,0:T(8,128)(2,1)S(1)}, u32[]{:S(2)}) copy-start(bf16[8,128,768]{2,1,0:T(8,128)(2,1)S(1)} %all_to_all.20) | copy-start | bytes 4718596
  201.7 10.7 %copy-start.72 = (bf16[1024,3072]{1,0:T(8,128)(2,1)}, bf16[1024,3072]{1,0:T(8,128)(2,1)S(1)}, u32[]{:S(2)}) copy-start(bf16[1024,3072]{1,0:T(8,128)(2,1)S(1)} %get-tuple-element.106) | copy-start | bytes 18874372
  212.4 6.9 copy-start.59
  212.4 6.9 copy-start.45
  212.4 25.4 %all-to-all-start.1 = ((bf16[8,128,768]{2,1,0:T(8,128)(2,1)}), bf16[8,128,768]{2,1,0:T(8,128)(2,1)}, u32[]{:S(2)}, u32[]{:S(2)}) async-start(bf16[8,128,768]{2,1,0:T(8,128)(2,1)} %bitcast.204), calls=%async_computation.1 | async-start | bytes 3145728 | tf_op jit(solution)/shard_map/all_to_all | solution.py:122
  219.3 28.2 %copy-start.48 = (f32[1024]{0:T(1024)}, f32[1024]{0:T(1024)S(1)}, u32[]{:S(2)}) copy-start(f32[1024]{0:T(1024)S(1)} %broadcast_select_fusion.1) | copy-start | bytes 12292
  286.2 16.4 %copy-start.26 = (bf16[8,128,768]{2,1,0:T(8,128)(2,1)}, bf16[8,128,768]{2,1,0:T(8,128)(2,1)S(1)}, u32[]{:S(2)}) copy-start(bf16[8,128,768]{2,1,0:T(8,128)(2,1)S(1)} %all_to_all.21) | copy-start | bytes 4718596
  312.1 4.5 copy-start.60
  312.1 25.5 %all-to-all-start.3 = ((bf16[8,128,768]{2,1,0:T(8,128)(2,1)}), bf16[8,128,768]{2,1,0:T(8,128)(2,1)}, u32[]{:S(2)}, u32[]{:S(2)}) async-start(bf16[8,128,768]{2,1,0:T(8,128)(2,1)} %bitcast.203), calls=%async_computation.3 | async-start | bytes 3145728 | tf_op jit(solution)/shard_map/all_to_all | solution.py:175
  316.5 478.0 %all-reduce.5.cloned.1.call-start = ((), (), s32[]{:S(2)}) async-start(), calls=%async_computation.8 | async-start | bytes 18874368 | tf_op jit(solution)/shard_map/psum | solution.py:251
  344.7 2.6 copy-start.29
  344.7 2.6 copy-start.33
  344.7 2.6 copy-start.36
  347.3 5.6 copy-start.44
  347.3 5.6 copy-start.6
  347.4 5.6 copy-start.12
  347.4 5.6 copy-start.17
  347.4 5.6 copy-start.49
  347.4 5.6 copy-start.61
  353.0 4.3 copy-start.13
  353.0 4.3 copy-start.57
  357.2 2.5 copy-start.25
  357.3 6.8 slice-start
  359.8 2.8 copy-start.67
  359.8 4.3 slice-start.1
  364.0 4.2 copy-start.71
  365.1 3.2 copy-start.23
  374.0 6.9 copy-start.8
  403.9 10.6 %copy-start.51 = (f32[12,512]{1,0:T(8,128)S(1)}, f32[12,512]{1,0:T(8,128)}, u32[]{:S(2)}) copy-start(f32[12,512]{1,0:T(8,128)} %get-tuple-element.120) | copy-start | bytes 73732
  403.9 10.6 %copy-start.52 = (f32[12,512]{1,0:T(8,128)S(1)}, f32[12,512]{1,0:T(8,128)}, u32[]{:S(2)}) copy-start(f32[12,512]{1,0:T(8,128)} %get-tuple-element.130) | copy-start | bytes 73732
  414.5 37.8 %copy-start.70 = (bf16[1,1024,12,64]{1,3,2,0:T(8,128)(2,1)}, bf16[1,1024,12,64]{1,3,2,0:T(8,128)(2,1)S(1)}, u32[]{:S(2)}) copy-start(bf16[1,1024,12,64]{1,3,2,0:T(8,128)(2,1)S(1)} %fusion.42) | copy-start | bytes 4718596
  414.5 21.9 %copy-start.9 = (bf16[1024,768]{0,1:T(8,128)(2,1)S(1)}, bf16[1024,768]{0,1:T(8,128)(2,1)}, u32[]{:S(2)}) copy-start(bf16[1024,768]{0,1:T(8,128)(2,1)} %copy.46) | copy-start | bytes 4718596
  436.4 8.7 %copy-start.16 = (bf16[1024,768]{0,1:T(8,128)(2,1)S(1)}, bf16[1024,768]{0,1:T(8,128)(2,1)}, u32[]{:S(2)}) copy-start(bf16[1024,768]{0,1:T(8,128)(2,1)} %copy.45) | copy-start | bytes 4718596
  436.4 8.7 %copy-start.18 = (f32[1,512,12,64]{1,3,2,0:T(8,128)S(1)}, f32[1,512,12,64]{1,3,2,0:T(8,128)}, u32[]{:S(2)}) copy-start(f32[1,512,12,64]{1,3,2,0:T(8,128)} %multiply_bitcast_fusion) | copy-start | bytes 4718596
  445.0 7.0 copy-start.20
  452.0 2.5 copy-start.3
  452.0 2.5 copy-start.31
  452.1 2.5 copy-start.38
  461.7 337.6 %reduce-scatter.5.cloned.1.call-start = ((), (), s32[]{:S(2)}) async-start(), calls=%async_computation.7 | async-start | bytes 5898240 | tf_op jit(solution)/shard_map/reduce_scatter | solution.py:151
  470.9 331.2 %reduce-scatter.3.cloned.1.call-start = ((), (), s32[]{:S(2)}) async-start(), calls=%async_computation.6 | async-start | bytes 5898240 | tf_op jit(solution)/shard_map/reduce_scatter | solution.py:164
  497.1 3.1 copy-start.42
  497.1 3.1 copy-start.4
  497.1 3.8 copy-start.7
  500.2 2.7 copy-start.11
  500.2 2.7 copy-start.14
  500.2 2.7 copy-start.40
  505.6 2.6 copy-start.62
  (17 other events, 27.1 us)
Sparse Core Ops, SparseCore 0:
  461.8 332.6 all-reduce.4
Sparse Core Ops, SparseCore 1:
  471.0 99.6 reduce-scatter.4
  572.9 97.5 reduce-scatter.2
where the time goes:
time: 819 us; the launch traced here: 813 us
  waiting for transfers between devices  280 us (34%)
  matrix products  220 us (27%)
  other arithmetic  109 us (13%)
  blocking collectives  94.4 us (12%)
  local copies, waits for them, and re-layouts  82.8 us (10%)
  between operations  17.3 us (2%)
  starting transfers between devices  8.87 us (1%)
    psum x1, waiting for transfers between devices, on_device(): lax.psum((input_weight_gradient, output_weight_gradient, gain_columns), (...  241 us
    psum x1, blocking collectives, on_device(): lax.psum((input_weight_gradient, output_weight_gradient, gain_columns), (...  43.2 us
    dot_general x1, matrix products, on_device(): upper = jnp.dot(flat, up_weight[0], preferred_element_type=jnp.float32)  35.7 us
    sub x1, other arithmetic, on_device(): weights = jnp.exp(scores - top)  34.4 us
    convert_element_type x2, other arithmetic, on_device(): score_gradient = (probs * (prob_gradient - inner)).astype(jnp.bfloat16)  28.8 us
    all_to_all x1, blocking collectives, on_device(): lax.all_to_all(outgoing, 'expert', split_axis=0, concat_axis=0, tiled=True)  26.6 us
    all_to_all x1, blocking collectives, on_device(): lax.all_to_all(gradient_outgoing, 'expert', split_axis=0, concat_axis=0,...  24.7 us
    dot_general x2, matrix products, on_device(): jnp.einsum('sqhd,skhd->shqk', incoming, values[:, :upto], preferred_eleme...  23.5 us
  transfers between devices with their start and end apart: 5, of which 3 were waited for; matrix products, arithmetic and copies ran while one was open for 7% of the time, Pallas kernels for 0%

commit v1 on v0

v1 whole, which is shorter than its diff:
```python
import functools

import jax
import jax.numpy as jnp
from jax import lax
from jax.experimental import pallas as pl
from jax.experimental.pallas import tpu as pltpu
from jax.sharding import PartitionSpec as P

HEADS = 12
EPS = 1e-05
EXCLUDED = -1e30
BF = jnp.bfloat16
F32 = jnp.float32
QUERY_ROWS = 256
GAIN_ROWS = 64


def dot(left, right, left_axis=1, right_axis=0):
    return lax.dot_general(
        left,
        right,
        (((left_axis,), (right_axis,)), ((), ())),
        preferred_element_type=F32,
    )


def params(limit=60):
    return pltpu.CompilerParams(vmem_limit_bytes=limit << 20)


def cost(flops, bytes_accessed, transcendentals=0):
    return pl.CostEstimate(
        flops=int(flops), bytes_accessed=int(bytes_accessed), transcendentals=int(transcendentals)
    )


def split_three(values):
    high = values.astype(BF)
    rest = values - high.astype(F32)
    middle = rest.astype(BF)
    return high, middle, (rest - middle.astype(F32)).astype(BF)


def normalise(values):
    average = jnp.mean(values, axis=-1, keepdims=True)
    centred = values - average
    variance = jnp.mean(centred * centred, axis=-1, keepdims=True)
    inverse = lax.rsqrt(variance + EPS)
    return centred * inverse, inverse


def norm_backward(normal, inverse, gain, gradient):
    scaled = gain * gradient
    first = jnp.mean(scaled, axis=-1, keepdims=True)
    second = jnp.mean(scaled * normal, axis=-1, keepdims=True)
    return (scaled - first - normal * second) * inverse


def selection(target_row, first, count):
    rows = lax.broadcasted_iota(jnp.int32, (count, target_row.shape[1]), 0) + first
    return jnp.where(rows == target_row, 1.0, 0.0).astype(BF)


def route_kernel(length_ref, expert_ref, cotangent_ref, out_ref, row_ref, column_ref, *, experts):
    step = pl.program_id(0)
    rows = cotangent_ref.shape[0]
    block = out_ref.shape[0]

    @pl.when(step == 0)
    def _():
        length = length_ref[0]
        position = lax.broadcasted_iota(jnp.int32, (1, rows), 1)
        named = jnp.where(position < length, expert_ref[...], -1)
        number = lax.broadcasted_iota(jnp.int32, (experts, rows), 0)
        onehot = jnp.where(number == named, 1.0, 0.0)
        before = lax.broadcasted_iota(jnp.int32, (rows, rows), 0)
        after = lax.broadcasted_iota(jnp.int32, (rows, rows), 1)
        earlier = jnp.where(before < after, 1.0, 0.0).astype(BF)
        counts = dot(onehot.astype(BF), earlier)
        slots = counts + (number * (rows // experts)).astype(F32)
        target = jnp.sum(onehot * slots, axis=0, keepdims=True)
        target = jnp.where(named >= 0, target, -1.0)
        row_ref[...] = jnp.broadcast_to(target, row_ref.shape).astype(jnp.int32)
        column_ref[...] = jnp.broadcast_to(target, (128, rows)).T.astype(jnp.int32)

    chosen = selection(row_ref[0:1, :], step * block, block)
    out_ref[...] = dot(chosen, cotangent_ref[...]).astype(BF)


def route(length, expert_index, cotangent, experts):
    rows, width = cotangent.shape
    block = 256
    return pl.pallas_call(
        functools.partial(route_kernel, experts=experts),
        out_shape=[
            jax.ShapeDtypeStruct((rows, width), BF),
            jax.ShapeDtypeStruct((8, rows), jnp.int32),
            jax.ShapeDtypeStruct((rows, 128), jnp.int32),
        ],
        grid_spec=pltpu.PrefetchScalarGridSpec(
            num_scalar_prefetch=1,
            grid=(rows // block,),
            in_specs=[
                pl.BlockSpec((1, rows), lambda i, l: (0, 0)),
                pl.BlockSpec((rows, width), lambda i, l: (0, 0)),
            ],
            out_specs=[
                pl.BlockSpec((block, width), lambda i, l: (i, 0)),
                pl.BlockSpec((8, rows), lambda i, l: (0, 0)),
                pl.BlockSpec((rows, 128), lambda i, l: (0, 0)),
            ],
        ),
        compiler_params=params(),
        cost_estimate=cost(2 * rows * rows * width, 4 * rows * width),
        name="route",
    )(length, expert_index.reshape(1, rows), cotangent)


def project_kernel(tokens_ref, weight_ref, gain_ref, shift_ref, out_ref):
    normal, _ = normalise(tokens_ref[...].astype(F32))
    normed = (normal * gain_ref[...] + shift_ref[...]).astype(BF)
    out_ref[...] = dot(normed, weight_ref[...]).astype(BF)


def project(tokens, weight, gain, shift):
    rows, width = tokens.shape
    columns = weight.shape[1]
    block = 256
    return pl.pallas_call(
        project_kernel,
        out_shape=jax.ShapeDtypeStruct((rows, columns), BF),
        grid=(rows // block,),
        in_specs=[
            pl.BlockSpec((block, width), lambda i: (i, 0)),
            pl.BlockSpec((width, columns), lambda i: (0, 0)),
            pl.BlockSpec((1, width), lambda i: (0, 0)),
            pl.BlockSpec((1, width), lambda i: (0, 0)),
        ],
        out_specs=pl.BlockSpec((block, columns), lambda i: (i, 0)),
        compiler_params=params(),
        cost_estimate=cost(2 * rows * width * columns, 2 * (rows + width) * columns),
        name="project",
    )(tokens, weight, gain, shift)


def attend_kernel(length_ref, query_ref, key_ref, value_ref, mixed_ref, total_ref, *, scale, half):
    rows = query_ref.shape[0]
    lane = lax.broadcasted_iota(jnp.int32, (1, 2 * half), 1)
    length = length_ref[0]
    zero, one = jnp.zeros((), BF), jnp.ones((), BF)
    for begin in range(0, rows, QUERY_ROWS):
        end = begin + QUERY_ROWS

        @pl.when(begin < length)
        def _(begin=begin, end=end):
            row = lax.broadcasted_iota(jnp.int32, (QUERY_ROWS, 1), 0) + begin
            limit = jnp.minimum(row, length - 1)
            column = lax.broadcasted_iota(jnp.int32, (QUERY_ROWS, QUERY_ROWS), 1) + begin
            allowed = column <= limit
            outs, totals = [], []
            for head in range(2):
                mine = (lane // half) == head
                other = half * (1 - head)
                query = jnp.where(mine, query_ref[begin:end, :] * jnp.asarray(scale, BF), zero)
                value = jnp.where(mine, value_ref[:end, :], jnp.where(lane == other, one, zero))
                scores = dot(query, key_ref[:end, :], 1, 1)
                last = jnp.where(allowed, scores[:, begin:], EXCLUDED)
                scores = jnp.concatenate([scores[:, :begin], last], axis=1) if begin else last
                top = jnp.max(scores, axis=1, keepdims=True)
                weights = jnp.exp(scores - top).astype(BF)
                out = dot(weights, value)
                total = out[:, other : other + 1]
                outs.append(out / total)
                totals.append(top + jnp.log(total))
            first = lane < half
            mixed_ref[begin:end, :] = jnp.where(first, outs[0], outs[1]).astype(BF)
            total_ref[begin:end, :] = jnp.where(first, totals[0], totals[1])

        @pl.when(begin >= length)
        def _(begin=begin, end=end):
            mixed_ref[begin:end, :] = jnp.zeros((QUERY_ROWS, 2 * half), BF)
            total_ref[begin:end, :] = jnp.zeros((QUERY_ROWS, 2 * half), F32)


def pair_specs(rows, wide, pairs, thirds):
    return [pl.BlockSpec((rows, wide), lambda i, l, o=o: (0, i + o * pairs)) for o in range(thirds)]


def attend(length, projected):
    rows, width = projected.shape[0], projected.shape[1] // 3
    size = width // HEADS
    pairs = HEADS // 2
    one = pl.BlockSpec((rows, 2 * size), lambda i, l: (0, i))
    return pl.pallas_call(
        functools.partial(attend_kernel, scale=size**-0.5, half=size),
        out_shape=[
            jax.ShapeDtypeStruct((rows, width), BF),
            jax.ShapeDtypeStruct((rows, width), F32),
        ],
        grid_spec=pltpu.PrefetchScalarGridSpec(
            num_scalar_prefetch=1,
            grid=(pairs,),
            in_specs=pair_specs(rows, 2 * size, pairs, 3),
            out_specs=[one, one],
        ),
        compiler_params=params(),
        cost_estimate=cost(
            16 * rows * rows * width, 12 * rows * width, HEADS * rows * rows // 2
        ),
        name="attend",
    )(length, projected, projected, projected)


def attend_back_kernel(
    length_ref,
    query_ref,
    key_ref,
    value_ref,
    mixed_ref,
    total_ref,
    incoming_ref,
    query_out,
    key_out,
    value_out,
    key_sum,
    value_sum,
    *,
    scale,
    half,
):
    rows = query_ref.shape[0]
    lane = lax.broadcasted_iota(jnp.int32, (1, 2 * half), 1)
    length = length_ref[0]
    zero, one = jnp.zeros((), BF), jnp.ones((), BF)
    key_sum[...] = jnp.zeros_like(key_sum)
    value_sum[...] = jnp.zeros_like(value_sum)
    for begin in range(0, rows, QUERY_ROWS):
        end = begin + QUERY_ROWS

        @pl.when(begin < length)
        def _(begin=begin, end=end):
            row = lax.broadcasted_iota(jnp.int32, (QUERY_ROWS, 1), 0) + begin
            column = lax.broadcasted_iota(jnp.int32, (QUERY_ROWS, QUERY_ROWS), 1) + begin
            allowed = (row <= column) & (row < length)
            incoming = incoming_ref[begin:end, :]
            product = incoming.astype(F32) * mixed_ref[begin:end, :].astype(F32)
            query_gradient = None
            for head in range(2):
                mine = (lane // half) == head
                other = half * (1 - head)
                ones = jnp.where((lane >= other) & (lane < other + 3), one, zero)

                def extend(base, column, mine=mine, other=other):
                    a, b, c = split_three(-column)
                    rest = jnp.where(lane == other + 2, c, zero)
                    rest = jnp.where(lane == other + 1, b, rest)
                    return jnp.where(mine, base, jnp.where(lane == other, a, rest))

                query = jnp.where(mine, query_ref[begin:end, :] * jnp.asarray(scale, BF), zero)
                grad = jnp.where(mine, incoming, zero)
                inner = jnp.sum(jnp.where(mine, product, 0.0), axis=1, keepdims=True)
                total = total_ref[begin:end, head * half : head * half + 1]
                key = key_ref[:end, :]
                scores = dot(jnp.where(mine, key, ones), extend(query, total), 1, 1)
                last = jnp.where(allowed, scores[begin:, :], EXCLUDED)
                scores = jnp.concatenate([scores[:begin, :], last], axis=0) if begin else last
                probs = jnp.exp(scores)
                centred = dot(
                    jnp.where(mine, value_ref[:end, :], ones), extend(grad, inner), 1, 1
                )
                score_gradient = (probs * centred).astype(BF)
                value_sum[:end, :] += dot(probs.astype(BF), grad)
                key_sum[:end, :] += dot(score_gradient, query)
                part = dot(score_gradient, jnp.where(mine, key, zero), 0, 0)
                query_gradient = part if query_gradient is None else query_gradient + part
            query_out[begin:end, :] = (query_gradient * scale).astype(BF)

        @pl.when(begin >= length)
        def _(begin=begin, end=end):
            query_out[begin:end, :] = jnp.zeros((QUERY_ROWS, 2 * half), BF)

    key_out[...] = key_sum[...].astype(BF)
    value_out[...] = value_sum[...].astype(BF)


def attend_back(length, projected, mixed, total, incoming):
    rows, width = projected.shape[0], projected.shape[1] // 3
    size = width // HEADS
    pairs = HEADS // 2
    one = pl.BlockSpec((rows, 2 * size), lambda i, l: (0, i))
    return pl.pallas_call(
        functools.partial(attend_back_kernel, scale=size**-0.5, half=size),
        out_shape=[jax.ShapeDtypeStruct((rows, width), BF)] * 3,
        grid_spec=pltpu.PrefetchScalarGridSpec(
            num_scalar_prefetch=1,
            grid=(pairs,),
            in_specs=pair_specs(rows, 2 * size, pairs, 3) + [one] * 3,
            out_specs=[one] * 3,
            scratch_shapes=[pltpu.VMEM((rows, 2 * size), F32)] * 2,
        ),
        compiler_params=params(),
        cost_estimate=cost(
            30 * rows * rows * width, 20 * rows * width, HEADS * rows * rows // 2
        ),
        name="attend_back",
    )(length, projected, projected, projected, mixed, total, incoming)


def picked_rows(column_ref, centroids_ref, capacity):
    experts, width = centroids_ref.shape
    pieces = [piece.astype(F32) for piece in split_three(centroids_ref[...])]
    rest = jnp.zeros((128 - 3 * experts, width), F32)
    table = jnp.concatenate(pieces + [rest], axis=0).astype(BF)
    target = column_ref[...]
    lane = lax.broadcasted_iota(jnp.int32, (1, 128), 1)
    low = jnp.where(lane < 3 * experts, (lane % experts) * capacity, 1 << 20)
    onehot = jnp.where((target >= low) & (target < low + capacity), 1.0, 0.0).astype(BF)
    return dot(onehot, table)


def present_rows(block_index, count, length):
    row = lax.broadcasted_iota(jnp.int32, (count, 1), 0) + block_index * count
    return jnp.where(row < length, 1.0, 0.0)


def hidden_kernel(
    length_ref,
    mixed_ref,
    tokens_ref,
    weight_ref,
    gain_ref,
    shift_ref,
    centroids_ref,
    row_ref,
    column_ref,
    residual_ref,
    gate_ref,
    out_ref,
    hidden_low,
    *,
    blocks,
):
    step = pl.program_id(0)
    count = mixed_ref.shape[0]

    @pl.when(step < blocks)
    def _():
        branch = dot(mixed_ref[...], weight_ref[...])
        mask = present_rows(step, count, length_ref[0])
        residual = tokens_ref[...].astype(F32) + mask * branch
        residual_ref[...] = residual
        normal, _ = normalise(residual)
        hidden = normal * gain_ref[...] + shift_ref[...]
        picked = picked_rows(column_ref, centroids_ref, row_ref.shape[1] // centroids_ref.shape[0])
        gate = jax.nn.sigmoid(jnp.sum(hidden * picked, axis=-1, keepdims=True))
        gate_ref[...] = jnp.broadcast_to(gate, gate_ref.shape)
        hidden_low[pl.ds(pl.multiple_of(step * count, count), count), :] = hidden.astype(BF)

    @pl.when(step >= blocks)
    def _():
        chosen = selection(row_ref[0:1, :], (step - blocks) * count, count)
        out_ref[...] = dot(chosen, hidden_low[...]).astype(BF)


def hidden_rows(length, mixed, tokens, weight, gain, shift, centroids, target_row, target_column):
    rows, width = tokens.shape
    experts = centroids.shape[0]
    block = 256
    blocks = rows // block
    early = lambda i, l: (jnp.minimum(i, blocks - 1), 0)
    late = lambda i, l: (jnp.maximum(i - blocks, 0), 0)
    still = lambda i, l: (0, 0)
    return pl.pallas_call(
        functools.partial(hidden_kernel, blocks=blocks),
        out_shape=[
            jax.ShapeDtypeStruct((rows, width), F32),
            jax.ShapeDtypeStruct((rows, 128), F32),
            jax.ShapeDtypeStruct((rows, width), BF),
        ],
        grid_spec=pltpu.PrefetchScalarGridSpec(
            num_scalar_prefetch=1,
            grid=(2 * blocks,),
            in_specs=[
                pl.BlockSpec((block, width), early),
                pl.BlockSpec((block, width), early),
                pl.BlockSpec((width, width), still),
                pl.BlockSpec((1, width), still),
                pl.BlockSpec((1, width), still),
                pl.BlockSpec((experts, width), still),
                pl.BlockSpec((8, rows), still),
                pl.BlockSpec((block, 128), early),
            ],
            out_specs=[
                pl.BlockSpec((block, width), early),
                pl.BlockSpec((block, 128), early),
                pl.BlockSpec((block, width), late),
            ],
            scratch_shapes=[pltpu.VMEM((rows, width), BF)],
        ),
        compiler_params=params(),
        cost_estimate=cost(2 * rows * (rows + width) * width, 12 * rows * width),
        name="hidden_rows",
    )(length, mixed, tokens, weight, gain, shift, centroids, target_row, target_column)


def expert_kernel(
    rows_ref,
    cotangent_ref,
    centroid_ref,
    up_ref,
    down_ref,
    produced_ref,
    back_ref,
    down_grad_ref,
    up_grad_ref,
    produced_sum,
    back_sum,
    transposed,
    gradient,
):
    step = pl.program_id(0)

    @pl.when(step == 0)
    def _():
        hidden = rows_ref[...]
        transposed[...] = hidden.T
        logit = jnp.sum(hidden.astype(F32) * centroid_ref[...], axis=-1, keepdims=True)
        gate = jax.nn.sigmoid(logit)
        gradient[...] = (gate * cotangent_ref[...].astype(F32)).astype(BF)
        produced_sum[...] = jnp.zeros_like(produced_sum)
        back_sum[...] = jnp.zeros_like(back_sum)

    upper = dot(rows_ref[...], up_ref[...])
    share = 0.5 + 0.5 * lax.erf(upper * (0.5**0.5))
    density = jnp.exp(upper * upper * -0.5) * 0.3989422804014327
    active = (upper * share).astype(BF)
    slope = share + upper * density
    active_gradient = dot(gradient[...], down_ref[...], 1, 1)
    upper_gradient = (active_gradient * slope).astype(BF)
    produced_sum[...] += dot(active, down_ref[...])
    down_grad_ref[...] = dot(active, gradient[...], 0, 0).astype(BF)
    back_sum[...] += dot(upper_gradient, up_ref[...], 1, 1)
    up_grad_ref[...] = dot(transposed[...], upper_gradient).astype(BF)

    @pl.when(step == pl.num_programs(0) - 1)
    def _():
        produced_ref[...] = produced_sum[...].astype(BF)
        back_ref[...] = back_sum[...].astype(BF)


def expert(rows, cotangent, centroid, up, down):
    count, width = rows.shape
    inner = up.shape[1]
    chunk = 512
    whole = pl.BlockSpec((count, width), lambda c: (0, 0))
    tall = pl.BlockSpec((chunk, width), lambda c: (c, 0))
    wide = pl.BlockSpec((width, chunk), lambda c: (0, c))
    return pl.pallas_call(
        expert_kernel,
        out_shape=[
            jax.ShapeDtypeStruct((count, width), BF),
            jax.ShapeDtypeStruct((count, width), BF),
            jax.ShapeDtypeStruct((inner, width), BF),
            jax.ShapeDtypeStruct((width, inner), BF),
        ],
        grid=(inner // chunk,),
        in_specs=[whole, whole, pl.BlockSpec((1, width), lambda c: (0, 0)), wide, tall],
        out_specs=[whole, whole, tall, wide],
        scratch_shapes=[
            pltpu.VMEM((count, width), F32),
            pltpu.VMEM((count, width), F32),
            pltpu.VMEM((width, count), BF),
            pltpu.VMEM((count, width), BF),
        ],
        compiler_params=params(),
        cost_estimate=cost(12 * count * width * inner, 8 * inner * width, 2 * count * inner),
        name="expert",
    )(rows, cotangent, centroid, up, down)


def combine_kernel(
    length_ref,
    produced_ref,
    back_ref,
    column_ref,
    cotangent_ref,
    residual_ref,
    gate_ref,
    gain_ref,
    centroids_ref,
    mixed_ref,
    weight_ref,
    layer_ref,
    residual_grad_ref,
    mixed_grad_ref,
    weight_grad_ref,
    gains_ref,
    weight_sum,
):
    step = pl.program_id(0)
    count, width = cotangent_ref.shape
    slots = produced_ref.shape[0]

    @pl.when(step == 0)
    def _():
        weight_sum[...] = jnp.zeros_like(weight_sum)
        gains_ref[...] = jnp.zeros_like(gains_ref)

    target = column_ref[:, 0:1]
    place = lax.broadcasted_iota(jnp.int32, (count, slots), 1)
    chosen = jnp.where(place == target, 1.0, 0.0).astype(BF)
    term = dot(chosen, produced_ref[...])
    back = dot(chosen, back_ref[...])
    mask = present_rows(step, count, length_ref[0])
    gate = gate_ref[:, 0:1]
    cotangent = cotangent_ref[...].astype(F32)
    residual = residual_ref[...]
    layer_ref[...] = (residual + mask * gate * term).astype(BF)
    along = jnp.sum(cotangent * term, axis=-1, keepdims=True)
    logit_gradient = mask * along * gate * (1.0 - gate)
    picked = picked_rows(column_ref, centroids_ref, slots // centroids_ref.shape[0])
    hidden_gradient = back + logit_gradient * picked
    normal, inverse = normalise(residual)
    gains_ref[0:1, :] += jnp.sum(hidden_gradient * normal, axis=0, keepdims=True)
    gains_ref[1:2, :] += jnp.sum(hidden_gradient, axis=0, keepdims=True)
    residual_gradient = cotangent + norm_backward(
        normal, inverse, gain_ref[...], hidden_gradient
    )
    residual_grad_ref[...] = residual_gradient
    branch_gradient = (mask * residual_gradient).astype(BF)
    mixed_grad_ref[...] = dot(branch_gradient, weight_ref[...], 1, 1).astype(BF)
    weight_sum[...] += dot(mixed_ref[...], branch_gradient, 0, 0)

    @pl.when(step == pl.num_programs(0) - 1)
    def _():
        weight_grad_ref[...] = weight_sum[...].astype(BF)


def combine(
    length, produced, back, target_column, cotangent, residual, gate, gain, centroids, mixed, weight
):
    rows, width = cotangent.shape
    experts = centroids.shape[0]
    block = 256
    part = pl.BlockSpec((block, width), lambda i, l: (i, 0))
    thin = pl.BlockSpec((block, 128), lambda i, l: (i, 0))
    still = lambda i, l: (0, 0)
    return pl.pallas_call(
        combine_kernel,
        out_shape=[
            jax.ShapeDtypeStruct((rows, width), BF),
            jax.ShapeDtypeStruct((rows, width), F32),
            jax.ShapeDtypeStruct((rows, width), BF),
            jax.ShapeDtypeStruct((width, width), BF),
            jax.ShapeDtypeStruct((8, width), F32),
        ],
        grid_spec=pltpu.PrefetchScalarGridSpec(
            num_scalar_prefetch=1,
            grid=(rows // block,),
            in_specs=[
                pl.BlockSpec((rows, width), still),
                pl.BlockSpec((rows, width), still),
                thin,
                part,
                part,
                thin,
                pl.BlockSpec((1, width), still),
                pl.BlockSpec((experts, width), still),
                part,
                pl.BlockSpec((width, width), still),
            ],
            out_specs=[
                part,
                part,
                part,
                pl.BlockSpec((width, width), still),
                pl.BlockSpec((8, width), still),
            ],
            scratch_shapes=[pltpu.VMEM((width, width), F32)],
        ),
        compiler_params=params(),
        cost_estimate=cost(4 * rows * (rows + width) * width, 24 * rows * width),
        name="combine",
    )(
        length,
        produced,
        back,
        target_column,
        cotangent,
        residual,
        gate,
        gain,
        centroids,
        mixed,
        weight,
    )


def project_back_kernel(
    query_ref,
    key_ref,
    value_ref,
    tokens_ref,
    residual_grad_ref,
    weight_ref,
    gain_ref,
    shift_ref,
    output_grad_ref,
    second_ref,
    input_grad_ref,
    packed_ref,
    weight_sum,
    gains,
    *,
    shares,
):
    step = pl.program_id(0)
    width = tokens_ref.shape[1]
    share = width // shares

    @pl.when(step == 0)
    def _():
        weight_sum[...] = jnp.zeros_like(weight_sum)
        gains[...] = jnp.zeros_like(gains)

    normal, inverse = normalise(tokens_ref[...].astype(F32))
    gain = gain_ref[...]
    normed = (normal * gain + shift_ref[...]).astype(BF)
    gradient = None
    for number, ref in enumerate((query_ref, key_ref, value_ref)):
        columns = slice(number * width, (number + 1) * width)
        part = dot(ref[...], weight_ref[:, columns], 1, 1)
        gradient = part if gradient is None else gradient + part
        weight_sum[number] += dot(normed, ref[...], 0, 0)
    gains[0:1, :] += jnp.sum(gradient * normal, axis=0, keepdims=True)
    gains[1:2, :] += jnp.sum(gradient, axis=0, keepdims=True)
    input_part = norm_backward(normal, inverse, gain, gradient)
    input_grad_ref[...] = (residual_grad_ref[...] + input_part).astype(BF)

    @pl.when(step == pl.num_programs(0) - 1)
    def _():
        rest = jnp.zeros((GAIN_ROWS - 4, width), F32)
        tail = jnp.concatenate([gains[0:2, :], second_ref[0:2, :], rest], axis=0).astype(BF)
        for number in range(shares):
            rows = slice(number * share, (number + 1) * share)
            for third in range(3):
                at = slice(third * share, (third + 1) * share)
                packed_ref[number, at, :] = weight_sum[third, rows, :].astype(BF)
            packed_ref[number, 3 * share : 4 * share, :] = output_grad_ref[rows, :]
            packed_ref[number, 4 * share :, :] = tail


def project_back(
    query, key, value, tokens, residual_grad, weight, gain, shift, output_grad, second, shares
):
    rows, width = tokens.shape
    block = 256
    packed_rows = 4 * (width // shares) + GAIN_ROWS
    part = pl.BlockSpec((block, width), lambda i: (i, 0))
    line = pl.BlockSpec((1, width), lambda i: (0, 0))
    return pl.pallas_call(
        functools.partial(project_back_kernel, shares=shares),
        out_shape=[
            jax.ShapeDtypeStruct((rows, width), BF),
            jax.ShapeDtypeStruct((shares, packed_rows, width), BF),
        ],
        grid=(rows // block,),
        in_specs=[
            part,
            part,
            part,
            part,
            part,
            pl.BlockSpec(weight.shape, lambda i: (0, 0)),
            line,
            line,
            pl.BlockSpec((width, width), lambda i: (0, 0)),
            pl.BlockSpec((8, width), lambda i: (0, 0)),
        ],
        out_specs=[part, pl.BlockSpec((shares, packed_rows, width), lambda i: (0, 0, 0))],
        scratch_shapes=[pltpu.VMEM((3, width, width), F32), pltpu.VMEM((8, width), F32)],
        compiler_params=params(),
        cost_estimate=cost(12 * rows * width * width, 40 * rows * width),
        name="project_back",
    )(query, key, value, tokens, residual_grad, weight, gain, shift, output_grad, second)


def line_scatter(parts, axis):
    n = lax.axis_size(axis)
    me = lax.axis_index(axis)

    def own(part, index):
        return lax.dynamic_index_in_dim(part, jnp.clip(index, 0, n - 1), 0, keepdims=False)

    results = []
    for part in parts:
        right = left = None
        for slot in range(n - 1):
            send = own(part, n - 1 - slot + me)
            send = send if right is None else send + right
            right = lax.ppermute(send, axis, [(z, z + 1) for z in range(slot + 1)])
            send = own(part, slot - (n - 1) + me)
            send = send if left is None else send + left
            left = lax.ppermute(send, axis, [(n - 1 - z, n - 2 - z) for z in range(slot + 1)])
        total = own(part, me).astype(F32)
        for arrived in (right, left):
            if arrived is not None:
                total = total + arrived.astype(F32)
        results.append(total)
    return results


def partner_pairs(axis, bit):
    return [(i, i ^ bit) for i in range(lax.axis_size(axis))]


def halve(values, axis, bit, dimension):
    upper = (lax.axis_index(axis) & bit) != 0
    size = values.shape[dimension] // 2
    low = lax.slice_in_dim(values, 0, size, axis=dimension)
    high = lax.slice_in_dim(values, size, 2 * size, axis=dimension)
    sent = lax.ppermute(jnp.where(upper, low, high), axis, partner_pairs(axis, bit))
    return jnp.where(upper, high, low) + sent


def unite(values, axis, bit, dimension):
    upper = (lax.axis_index(axis) & bit) != 0
    other = lax.ppermute(values, axis, partner_pairs(axis, bit))
    low = jnp.where(upper, other, values)
    high = jnp.where(upper, values, other)
    return jnp.concatenate([low, high], axis=dimension)


def on_device(
    tokens,
    lengths,
    expert_index,
    centroids,
    input_weight,
    output_weight,
    first_gain,
    first_shift,
    second_gain,
    second_shift,
    up_weight,
    down_weight,
    cotangent,
):
    rows, width = tokens.shape
    experts = centroids.shape[0]
    capacity = rows // experts
    shares = lax.axis_size("dp")
    share = width // shares
    line = lambda vector: vector.reshape(1, width)
    exchange = lambda values: lax.all_to_all(
        values.reshape(experts, capacity, width), "expert", split_axis=0, concat_axis=0, tiled=True
    ).reshape(rows, width)

    outgoing_cotangent, target_row, target_column = route(
        lengths, expert_index, cotangent, experts
    )
    arrived_cotangent = exchange(outgoing_cotangent)
    projected = project(tokens, input_weight, line(first_gain), line(first_shift))
    mixed, total = attend(lengths, projected)
    residual, gate, outgoing = hidden_rows(
        lengths,
        mixed,
        tokens,
        output_weight,
        line(second_gain),
        line(second_shift),
        centroids,
        target_row,
        target_column,
    )
    arrived = exchange(outgoing)
    centroid = lax.dynamic_slice_in_dim(centroids, lax.axis_index("expert"), 1, 0)
    produced, back, down_grad, up_grad = expert(
        arrived, arrived_cotangent, centroid, up_weight[0], down_weight[0]
    )
    returned = exchange(produced)
    returned_back = exchange(back)
    inner = up_weight.shape[2]
    down_share, up_share = line_scatter(
        [
            down_grad.reshape(shares, inner // shares, width),
            up_grad.reshape(shares, share, inner),
        ],
        "dp",
    )
    layer_output, residual_grad, mixed_grad, output_grad, second_gains = combine(
        lengths,
        returned,
        returned_back,
        target_column,
        cotangent,
        residual,
        gate,
        line(second_gain),
        centroids,
        mixed,
        output_weight,
    )
    query, key, value = attend_back(lengths, projected, mixed, total, mixed_grad)
    input_gradient, packed = project_back(
        query,
        key,
        value,
        tokens,
        residual_grad,
        input_weight,
        line(first_gain),
        line(first_shift),
        output_grad,
        second_gains,
        shares,
    )
    bits = []
    bit = 1
    while bit < experts:
        bits.append((bit, 2 if bit == 1 else 1))
        bit *= 2
    for bit, dimension in bits:
        packed = halve(packed, "expert", bit, dimension)
    summed = line_scatter([packed], "dp")[0].astype(BF)
    for bit, dimension in reversed(bits):
        summed = unite(summed, "expert", bit, dimension - 1)
    summed = summed.astype(F32)
    input_share = jnp.concatenate(
        [summed[number * share : (number + 1) * share] for number in range(3)], axis=1
    )
    output_share = summed[3 * share : 4 * share]
    gains = lax.dynamic_slice_in_dim(
        summed[4 * share : 4 * share + 4], lax.axis_index("dp") * share, share, 1
    )
    return (
        layer_output,
        input_gradient,
        input_share,
        output_share,
        gains[0],
        gains[1],
        gains[2],
        gains[3],
        up_share[None],
        down_share[None],
    )


def solution(mesh):
    both = P(("dp", "expert"))
    rows = P(("dp", "expert"), None)
    weights = P("expert", None, None)
    return jax.shard_map(
        on_device,
        mesh=mesh,
        in_specs=(rows, both, both, P(), P(), P(), P(), P(), P(), P(), weights, weights, rows),
        out_specs=(
            rows,
            rows,
            P("dp", None),
            P("dp", None),
            P("dp"),
            P("dp"),
            P("dp"),
            P("dp"),
            P("expert", "dp", None),
            P("expert", "dp", None),
        ),
        check_vma=False,
    )
```

time: 819 us -> 502 us (0.61)
  matrix products: 220 us -> 0 us
  waiting for transfers between devices: 280 us -> 151 us
  Pallas kernels: 0 us -> 120 us
  starting transfers between devices: 8.87 us -> 104 us
  other arithmetic: 109 us -> 37.2 us
  local copies, waits for them, and re-layouts: 82.8 us -> 15.1 us
  blocking collectives: 94.4 us -> 64.5 us
  between operations: 17.3 us -> 1.68 us
    psum x1 -> x0, waiting for transfers between devices: 241 us -> none  [on_device(): lax.psum((input_weight_gradient, output_weight_gradient, gain_columns), (...]
    dot_general x24 -> x0, matrix products: 209 us -> none  [the longest x1 35.7 us: on_device(): upper = jnp.dot(flat, up_weight[0], preferred_element_type=jnp.float32)]
    pallas_call x0 -> x8, Pallas kernels: none -> 120 us  [the longest x1 37.3 us: expert(): pl.pallas_call(expert_kernel, out_shape=[jax.ShapeDtypeStruct((count, wid...]
    ppermute x0 -> x24, waiting for transfers between devices: none -> 111 us  [the longest x9 63 us: line_scatter(): right = lax.ppermute(send, axis, [(z, z + 1) for z in range(slot + 1)])]
    ppermute x0 -> x24, starting transfers between devices: none -> 96.6 us  [the longest x9 63.8 us: line_scatter(): right = lax.ppermute(send, axis, [(z, z + 1) for z in range(slot + 1)])]
    psum x1 -> x0, blocking collectives: 43.2 us -> none  [on_device(): lax.psum((input_weight_gradient, output_weight_gradient, gain_columns), (...]
    convert_element_type x7 -> x2, other arithmetic: 37.8 us -> 0.26 us  [the longest x1 0.18 us: on_device(): summed = summed.astype(F32)]
    sub x1 -> x0, other arithmetic: 34.4 us -> none  [on_device(): weights = jnp.exp(scores - top)]
  transfers between devices with their start and end apart: 5 -> 26, of which waited for: 3 -> 12; matrix products, arithmetic and copies ran while one was open for 7% -> 8% of each run, Pallas kernels for 0% -> 0%
where the time goes in v1:
time: 502 us; the launch traced here: 493 us
  waiting for transfers between devices  151 us (30%)
  Pallas kernels  120 us (24%)
  starting transfers between devices  104 us (21%)
  blocking collectives  64.5 us (13%)
  other arithmetic  37.2 us (7%)
  local copies, waits for them, and re-layouts  15.1 us (3%)
    all_to_all x2, blocking collectives, on_device(): lax.all_to_all(values.reshape(experts, capacity, width), 'expert', split_...  64.5 us
    ppermute x9, starting transfers between devices, line_scatter(): right = lax.ppermute(send, axis, [(z, z + 1) for z in range(slot + 1)])  63.8 us
    ppermute x9, waiting for transfers between devices, line_scatter(): right = lax.ppermute(send, axis, [(z, z + 1) for z in range(slot + 1)])  63 us
    all_to_all x2, waiting for transfers between devices, on_device(): lax.all_to_all(values.reshape(experts, capacity, width), 'expert', split_...  40.2 us
    pallas_call x1, Pallas kernels, expert(): pl.pallas_call(expert_kernel, out_shape=[jax.ShapeDtypeStruct((count, wid...  37.3 us
    ppermute x9, waiting for transfers between devices, line_scatter(): lax.ppermute(send, axis, [(n - 1 - z, n - 2 - z) for z in range(slot + 1)])  33.8 us
    pallas_call x1, Pallas kernels, project_back(): pl.pallas_call(functools.partial(project_back_kernel, shares=shares), out...  16.6 us
    pallas_call x1, Pallas kernels, attend_back(): pl.pallas_call(functools.partial(attend_back_kernel, scale=size ** (-0.5)...  15.5 us
  transfers between devices with their start and end apart: 26, of which 12 were waited for; matrix products, arithmetic and copies ran while one was open for 8% of the time, Pallas kernels for 0%

profile of v1, /device:TPU:0, one launch (start us, length us, event | category | flops | bytes accessed | tf_op | source)
XLA Modules:
  0.0 493.2 jit_solution(15680031271784619257)
XLA Ops:
  1.3 1.3 reshape.74.gain_ref
  2.6 1.3 reshape.75.shift_ref
  3.8 1.3 reshape.76.gain_ref
  5.1 1.3 reshape.77.shift_ref
  6.4 8.4 %project.1.query_ref.key_ref.value_ref = bf16[1024,2304]{1,0:T(8,128)(2,1)} custom-call(bf16[1024,768]{1,0:T(8,128)(2,1)} %tokens_ref.5, bf16[768,2304]{1,0:T(8,128)(2,1)} %weight_ref.7, f32[1,768]{1,0:T(1,128)} %reshape.74.gain_ref, f32[1,768]{1,0:T(1,128)} %reshape.75.shift_ref), custom_call_target="tpu_custom_call" | custom-call | flops 3623878656 | bytes 8257536 | tf_op jit(solution)/shard_map/project/pallas_call | solution.py:130
  14.8 12.4 %attend.1 = (bf16[1024,768]{1,0:T(8,128)(2,1)}, f32[1024,768]{1,0:T(8,128)}) custom-call(s32[1]{0:T(128)S(6)} %copy.23.length_ref, bf16[1024,2304]{1,0:T(8,128)(2,1)} %project.1.query_ref.key_ref.value_ref, bf16[1024,2304]{1,0:T(8,128)(2,1)} %project.1.query_ref.key_ref.value_ref, bf16[1024,2304]{1,0:T(8,128)(2,1)} %project.1.query_ref.key_ref.value_ref), custom_call_target="tpu_custom_call" | custom-call | flops 12884901888 | bytes 9437184 | tf_op jit(solution)/shard_map/attend/pallas_call | solution.py:195
  27.2 5.1 %route.1 = (bf16[1024,768]{1,0:T(8,128)(2,1)}, s32[8,1024]{1,0:T(8,128)}, s32[1024,128]{1,0:T(8,128)}) custom-call(s32[1]{0:T(128)S(6)} %copy.23.length_ref, s32[1,1024]{1,0:T(1,128)} %bitcast.92, bf16[1024,768]{1,0:T(8,128)(2,1)} %cotangent_ref.3), custom_call_target="tpu_custom_call" | custom-call | flops 1610612736 | bytes 3145728 | tf_op jit(solution)/shard_map/route/pallas_call | solution.py:94
  32.3 9.9 %hidden_rows.1 = (f32[1024,768]{1,0:T(8,128)}, f32[1024,128]{1,0:T(8,128)}, bf16[1024,768]{1,0:T(8,128)(2,1)}) custom-call(s32[1]{0:T(128)S(6)} %copy.23.length_ref, bf16[1024,768]{1,0:T(8,128)(2,1)} %get-tuple-element.32.mixed_ref, bf16[1024,768]{1,0:T(8,128)(2,1)} %tokens_ref.5, bf16[768,768]{1,0:T(8,128)(2,1)} %weight_ref.6, f32[1,768]{1,0:T(1,128)} %reshape.76.gain_ref, ...), custom_call_target="tpu_custom_call" | custom-call | flops 2818572288 | bytes 9437184 | tf_op jit(solution)/shard_map/hidden_rows/pallas_call | solution.py:374
  42.2 39.2 %all_to_all.20 = bf16[8,128,768]{2,1,0:T(8,128)(2,1)} all-to-all(bf16[8,128,768]{2,1,0:T(8,128)(2,1)} %bitcast.85), channel_id=1, replica_groups=mesh['dp'=4,'expert'=8] {'expert'}, dimensions={0} | all-to-all | bytes 3145728 | tf_op jit(solution)/shard_map/all_to_all | solution.py:756
  81.4 3.8 all-to-all-start.1
  85.1 1.3 constant_dynamic-slice_fusion.centroid_ref
  86.5 19.4 %all-to-all-done.1 = bf16[8,128,768]{2,1,0:T(8,128)(2,1)S(1)} async-done(((bf16[8,128,768]{2,1,0:T(8,128)(2,1)}), bf16[8,128,768]{2,1,0:T(8,128)(2,1)S(1)}, u32[]{:S(2)}, u32[]{:S(2)}) %all-to-all-start.1) | async-done | bytes 1572896 | tf_op jit(solution)/shard_map/all_to_all | solution.py:756
  107.0 37.3 %expert.1 = (bf16[1024,768]{1,0:T(8,128)(2,1)}, bf16[1024,768]{1,0:T(8,128)(2,1)}, bf16[3072,768]{1,0:T(8,128)(2,1)}, bf16[768,3072]{1,0:T(8,128)(2,1)}) custom-call(bf16[1024,768]{1,0:T(8,128)(2,1)} %bitcast.80, bf16[1024,768]{1,0:T(8,128)(2,1)} %bitcast.81, f32[1,768]{1,0:T(1,128)} %constant_dynamic-slice_fusion.centroid_ref, bf16[768,3072]{1,0:T(8,128)(2,1)} %bitcast.90, ...), custom_call_target="tpu_custom_call" | custom-call | flops 28991029248 | bytes 18874368 | tf_op jit(solution)/shard_map/expert/pallas_call | solution.py:459
  144.4 25.3 %all_to_all.21 = bf16[8,128,768]{2,1,0:T(8,128)(2,1)} all-to-all(bf16[8,128,768]{2,1,0:T(8,128)(2,1)} %bitcast.84), channel_id=1, replica_groups=mesh['dp'=4,'expert'=8] {'expert'}, dimensions={0} | all-to-all | bytes 3145728 | tf_op jit(solution)/shard_map/all_to_all | solution.py:756
  169.6 3.8 all-to-all-start.2
  173.5 20.7 %all-to-all-done.2 = bf16[8,128,768]{2,1,0:T(8,128)(2,1)S(1)} async-done(((bf16[8,128,768]{2,1,0:T(8,128)(2,1)}), bf16[8,128,768]{2,1,0:T(8,128)(2,1)S(1)}, u32[]{:S(2)}, u32[]{:S(2)}) %all-to-all-start.2) | async-done | bytes 1572896 | tf_op jit(solution)/shard_map/all_to_all | solution.py:756
  195.3 14.4 %combine.1 = (bf16[1024,768]{1,0:T(8,128)(2,1)}, f32[1024,768]{1,0:T(8,128)}, bf16[1024,768]{1,0:T(8,128)(2,1)}, bf16[768,768]{1,0:T(8,128)(2,1)}, f32[8,768]{1,0:T(8,128)}) custom-call(s32[1]{0:T(128)S(6)} %copy.23.length_ref, bf16[1024,768]{1,0:T(8,128)(2,1)} %bitcast.83, bf16[1024,768]{1,0:T(8,128)(2,1)} %bitcast.82, ...), custom_call_target="tpu_custom_call" | custom-call | flops 5637144576 | bytes 18874368 | tf_op jit(solution)/shard_map/combine/pallas_call | solution.py:549
  209.7 15.5 %attend_back.1 = (bf16[1024,768]{1,0:T(8,128)(2,1)}, bf16[1024,768]{1,0:T(8,128)(2,1)}, bf16[1024,768]{1,0:T(8,128)(2,1)}) custom-call(s32[1]{0:T(128)S(6)} %copy.23.length_ref, bf16[1024,2304]{1,0:T(8,128)(2,1)} %project.1.query_ref.key_ref.value_ref, bf16[1024,2304]{1,0:T(8,128)(2,1)} %project.1.query_ref.key_ref.value_ref, ...), custom_call_target="tpu_custom_call" | custom-call | flops 24159191040 | bytes 15728640 | tf_op jit(solution)/shard_map/attend_back/pallas_call | solution.py:292
  225.2 16.6 %project_back.1 = (bf16[1024,768]{1,0:T(8,128)(2,1)}, bf16[4,832,768]{2,1,0:T(8,128)(2,1)}) custom-call(bf16[1024,768]{1,0:T(8,128)(2,1)} %get-tuple-element.44.query_ref, bf16[1024,768]{1,0:T(8,128)(2,1)} %get-tuple-element.45.key_ref, bf16[1024,768]{1,0:T(8,128)(2,1)} %get-tuple-element.46.value_ref, bf16[1024,768]{1,0:T(8,128)(2,1)} %tokens_ref.5, ...), custom_call_target="tpu_custom_call" | custom-call | flops 7247757312 | bytes 31457280 | tf_op jit(solution)/shard_map/project_back/pallas_call | solution.py:662
  241.8 2.8 broadcast_select_fusion
  244.7 3.2 dynamic-slice_bitcast_fusion.1
  247.9 13.2 %collective-permute-start.18 = (bf16[768,768]{1,0:T(8,128)(2,1)}, bf16[768,768]{1,0:T(8,128)(2,1)}, u32[]{:S(2)}, u32[]{:S(2)}) collective-permute-start(bf16[768,768]{1,0:T(8,128)(2,1)} %get-tuple-element.56), channel_id=1, source_target_pairs={{0,8},{1,9},{2,10},{3,11},{4,12},{5,13},{6,14},{7,15}} | collective-permute-start | bytes 3538952 | tf_op jit(solution)/shard_map/ppermute | solution.py:702
  261.1 3.6 select_add_fusion
  264.7 1.2 broadcast_select_fusion.1
  265.9 9.0 %collective-permute-start.1 = (bf16[4,416,384]{2,1,0:T(8,128)(2,1)}, bf16[4,416,384]{2,1,0:T(8,128)(2,1)}, u32[]{:S(2)}, u32[]{:S(2)}) collective-permute-start(bf16[4,416,384]{2,1,0:T(8,128)(2,1)} %broadcast_select_fusion.1), channel_id=1, source_target_pairs={{0,2},{1,3},{2,0},{3,1},{4,6},{5,7},{6,4},{7,5},{8,10},{9,11},{10,... | collective-permute-start | bytes 3833864 | tf_op jit(solution)/shard_map/ppermute | solution.py:723
  274.9 1.6 dynamic-slice_bitcast_fusion.3
  276.5 2.3 collective-permute-start.12
  278.8 1.7 collective-permute-start.21
  280.5 1.7 collective-permute-start.15
  282.2 4.4 collective-permute-done.18
  286.6 2.8 bitcast_add_fusion.2
  289.4 5.4 %collective-permute-start.19 = (bf16[768,768]{1,0:T(8,128)(2,1)}, bf16[768,768]{1,0:T(8,128)(2,1)}, u32[]{:S(2)}, u32[]{:S(2)}) collective-permute-start(bf16[768,768]{1,0:T(8,128)(2,1)} %bitcast_add_fusion.2), channel_id=1, source_target_pairs={{0,8},{8,16},{1,9},{9,17},{2,10},{10,18},{3,11},{11,19},{4,12},{12... | collective-permute-start | bytes 3538952 | tf_op jit(solution)/shard_map/ppermute | solution.py:702
  294.8 9.1 %collective-permute-done.1 = bf16[4,416,384]{2,1,0:T(8,128)(2,1)} collective-permute-done((bf16[4,416,384]{2,1,0:T(8,128)(2,1)}, bf16[4,416,384]{2,1,0:T(8,128)(2,1)}, u32[]{:S(2)}, u32[]{:S(2)}) %collective-permute-start.1) | collective-permute-done | bytes 1277984 | tf_op jit(solution)/shard_map/ppermute | solution.py:723
  303.9 1.5 select_add_fusion.1
  305.5 1.8 collective-permute-start.2
  307.3 4.6 collective-permute-done.12
  311.9 1.7 bitcast_add_fusion.6
  313.7 4.5 collective-permute-start.13
  318.2 3.7 collective-permute-done.2
  321.9 1.7 select_add_fusion.2
  323.6 1.4 collective-permute-start.3
  325.1 12.1 %collective-permute-done.19 = bf16[768,768]{1,0:T(8,128)(2,1)} collective-permute-done((bf16[768,768]{1,0:T(8,128)(2,1)}, bf16[768,768]{1,0:T(8,128)(2,1)}, u32[]{:S(2)}, u32[]{:S(2)}) %collective-permute-start.19) | collective-permute-done | bytes 1179680 | tf_op jit(solution)/shard_map/ppermute | solution.py:702
  337.2 4.0 bitcast_add_fusion.3
  341.2 1.7 collective-permute-start.22
  343.5 21.8 %collective-permute-done.3 = bf16[208,384]{1,0:T(8,128)(2,1)S(1)} collective-permute-done((bf16[208,384]{1,0:T(8,128)(2,1)S(1)}, bf16[208,384]{1,0:T(8,128)(2,1)S(1)}, u32[]{:S(2)}, u32[]{:S(2)}) %collective-permute-start.3) | collective-permute-done | bytes 159776 | tf_op jit(solution)/shard_map/ppermute | solution.py:702
  365.4 4.4 collective-permute-start.4
  369.8 2.9 bitcast_add_fusion.7
  372.8 1.7 collective-permute-start.16
  375.2 3.7 collective-permute-start.20
  378.9 4.5 collective-permute-start.14
  383.5 24.4 %collective-permute-start.5 = (bf16[208,384]{1,0:T(8,128)(2,1)S(1)}, bf16[208,384]{1,0:T(8,128)(2,1)S(1)}, u32[]{:S(2)}, u32[]{:S(2)}) collective-permute-start(bf16[208,384]{1,0:T(8,128)(2,1)S(1)} %get-tuple-element.70), channel_id=1, source_target_pairs={{0,8},{8,16},{16,24},{1,9},{9,17},{17,25},{2,10},{10,18},{18,26},{... | collective-permute-start | bytes 479240 | tf_op jit(solution)/shard_map/ppermute | solution.py:702
  407.9 1.3 collective-permute-start.8
  409.2 2.8 bitcast_add_fusion.1
  412.0 20.0 %collective-permute-done.5 = bf16[208,384]{1,0:T(8,128)(2,1)S(1)} collective-permute-done((bf16[208,384]{1,0:T(8,128)(2,1)S(1)}, bf16[208,384]{1,0:T(8,128)(2,1)S(1)}, u32[]{:S(2)}, u32[]{:S(2)}) %collective-permute-start.5) | collective-permute-done | bytes 159776 | tf_op jit(solution)/shard_map/ppermute | solution.py:702
  432.1 1.3 collective-permute-start.23
  433.5 2.8 bitcast_add_fusion.5
  436.3 1.3 collective-permute-start.17
  437.6 1.2 collective-permute-done.9
  438.9 9.8 %collective-permute-start.10 = (bf16[416,384]{1,0:T(8,128)(2,1)S(1)}, bf16[416,384]{1,0:T(8,128)(2,1)S(1)}, u32[]{:S(2)}, u32[]{:S(2)}) collective-permute-start(bf16[416,384]{1,0:T(8,128)(2,1)S(1)} %pad_maximum_fusion.2), channel_id=1, source_target_pairs={{0,2},{1,3},{2,0},{3,1},{4,6},{5,7},{6,4},{7,5},{8,10},{9,11},{10,... | collective-permute-start | bytes 958472 | tf_op jit(solution)/shard_map/ppermute | solution.py:729
  448.6 15.0 %collective-permute-done.23 = bf16[768,768]{1,0:T(8,128)(2,1)} collective-permute-done((bf16[768,768]{1,0:T(8,128)(2,1)}, bf16[768,768]{1,0:T(8,128)(2,1)}, u32[]{:S(2)}, u32[]{:S(2)}) %collective-permute-start.23) | collective-permute-done | bytes 1179680 | tf_op jit(solution)/shard_map/ppermute | solution.py:705
  463.6 3.4 fusion.1
  467.3 18.8 %collective-permute-done.17 = bf16[192,3072]{1,0:T(8,128)(2,1)} collective-permute-done((bf16[192,3072]{1,0:T(8,128)(2,1)}, bf16[192,3072]{1,0:T(8,128)(2,1)}, u32[]{:S(2)}, u32[]{:S(2)}) %collective-permute-start.17) | collective-permute-done | bytes 1179680 | tf_op jit(solution)/shard_map/ppermute | solution.py:705
  486.1 3.6 fusion.3
  491.8 1.3 pad_maximum_fusion
  (50 shorter events, 6.5 us)
Async XLA Ops:
  81.4 24.5 %all-to-all-start.1 = ((bf16[8,128,768]{2,1,0:T(8,128)(2,1)}), bf16[8,128,768]{2,1,0:T(8,128)(2,1)S(1)}, u32[]{:S(2)}, u32[]{:S(2)}) async-start(bf16[8,128,768]{2,1,0:T(8,128)(2,1)} %bitcast.3), calls=%async_computation.1 | async-start | bytes 3145728 | tf_op jit(solution)/shard_map/all_to_all | solution.py:756
  105.9 1.1 copy-start.1
  169.6 24.5 %all-to-all-start.2 = ((bf16[8,128,768]{2,1,0:T(8,128)(2,1)}), bf16[8,128,768]{2,1,0:T(8,128)(2,1)S(1)}, u32[]{:S(2)}, u32[]{:S(2)}) async-start(bf16[8,128,768]{2,1,0:T(8,128)(2,1)} %bitcast.7), calls=%async_computation.2 | async-start | bytes 3145728 | tf_op jit(solution)/shard_map/all_to_all | solution.py:756
  194.2 1.1 copy-start.2
  244.6 16.5 %collective-permute-start = (bf16[4,832,384]{2,1,0:T(8,128)(2,1)S(1)}, bf16[4,832,384]{2,1,0:T(8,128)(2,1)}, u32[]{:S(2)}, u32[]{:S(2)}) collective-permute-start(bf16[4,832,384]{2,1,0:T(8,128)(2,1)S(1)} %broadcast_select_fusion), channel_id=1, source_target_pairs={{0,1},{1,0},{2,3},{3,2},{4,5},{5,4},{6,7},{7,6},{8,9},{9,8},{10,11... | collective-permute-start | bytes 7667720 | tf_op jit(solution)/shard_map/ppermute | solution.py:723
  247.9 27.0 %slice-start = ((s8[4718592]{0:T(1024)(128)(4,1)}), s8[4194304]{0:T(1024)(128)(4,1)S(1)}, s32[]{:S(2)}) async-start(s8[4718592]{0:T(1024)(128)(4,1)} %bitcast.69), calls=%async_computation.4 | async-start | bytes 8388608
  247.9 27.0 %slice-start.1 = ((s8[4718592]{0:T(1024)(128)(4,1)}), s8[524288]{0:T(1024)(128)(4,1)S(1)}, s32[]{:S(2)}) async-start(s8[4718592]{0:T(1024)(128)(4,1)} %bitcast.69), calls=%async_computation.5 | async-start | bytes 1048576
  247.9 38.7 %collective-permute-start.18 = (bf16[768,768]{1,0:T(8,128)(2,1)}, bf16[768,768]{1,0:T(8,128)(2,1)}, u32[]{:S(2)}, u32[]{:S(2)}) collective-permute-start(bf16[768,768]{1,0:T(8,128)(2,1)} %get-tuple-element.56), channel_id=1, source_target_pairs={{0,8},{1,9},{2,10},{3,11},{4,12},{5,13},{6,14},{7,15}} | collective-permute-start | bytes 3538952 | tf_op jit(solution)/shard_map/ppermute | solution.py:702
  265.9 38.0 %collective-permute-start.1 = (bf16[4,416,384]{2,1,0:T(8,128)(2,1)}, bf16[4,416,384]{2,1,0:T(8,128)(2,1)}, u32[]{:S(2)}, u32[]{:S(2)}) collective-permute-start(bf16[4,416,384]{2,1,0:T(8,128)(2,1)} %broadcast_select_fusion.1), channel_id=1, source_target_pairs={{0,2},{1,3},{2,0},{3,1},{4,6},{5,7},{6,4},{7,5},{8,10},{9,11},{10,... | collective-permute-start | bytes 3833864 | tf_op jit(solution)/shard_map/ppermute | solution.py:723
  276.5 35.5 %collective-permute-start.12 = (bf16[192,3072]{1,0:T(8,128)(2,1)}, bf16[192,3072]{1,0:T(8,128)(2,1)}, u32[]{:S(2)}, u32[]{:S(2)}) collective-permute-start(bf16[192,3072]{1,0:T(8,128)(2,1)} %get-tuple-element.60), channel_id=1, source_target_pairs={{0,8},{1,9},{2,10},{3,11},{4,12},{5,13},{6,14},{7,15}} | collective-permute-start | bytes 3538952 | tf_op jit(solution)/shard_map/ppermute | solution.py:702
  278.8 46.3 %collective-permute-start.21 = (bf16[768,768]{1,0:T(8,128)(2,1)}, bf16[768,768]{1,0:T(8,128)(2,1)}, u32[]{:S(2)}, u32[]{:S(2)}) collective-permute-start(bf16[768,768]{1,0:T(8,128)(2,1)} %get-tuple-element.57), channel_id=1, source_target_pairs={{24,16},{25,17},{26,18},{27,19},{28,20},{29,21},{30,22},{31,23}} | collective-permute-start | bytes 3538952 | tf_op jit(solution)/shard_map/ppermute | solution.py:705
  280.5 89.3 %collective-permute-start.15 = (bf16[192,3072]{1,0:T(8,128)(2,1)}, bf16[192,3072]{1,0:T(8,128)(2,1)}, u32[]{:S(2)}, u32[]{:S(2)}) collective-permute-start(bf16[192,3072]{1,0:T(8,128)(2,1)} %get-tuple-element.61), channel_id=1, source_target_pairs={{24,16},{25,17},{26,18},{27,19},{28,20},{29,21},{30,22},{31,23}} | collective-permute-start | bytes 3538952 | tf_op jit(solution)/shard_map/ppermute | solution.py:705
  289.4 47.8 %collective-permute-start.19 = (bf16[768,768]{1,0:T(8,128)(2,1)}, bf16[768,768]{1,0:T(8,128)(2,1)}, u32[]{:S(2)}, u32[]{:S(2)}) collective-permute-start(bf16[768,768]{1,0:T(8,128)(2,1)} %bitcast_add_fusion.2), channel_id=1, source_target_pairs={{0,8},{8,16},{1,9},{9,17},{2,10},{10,18},{3,11},{11,19},{4,12},{12... | collective-permute-start | bytes 3538952 | tf_op jit(solution)/shard_map/ppermute | solution.py:702
  305.4 8.3 %copy-start = (bf16[4,416,384]{2,1,0:T(8,128)(2,1)}, bf16[4,416,384]{2,1,0:T(8,128)(2,1)S(1)}, u32[]{:S(2)}) copy-start(bf16[4,416,384]{2,1,0:T(8,128)(2,1)S(1)} %select_add_fusion.1) | copy-start | bytes 3833860
  305.5 16.4 %collective-permute-start.2 = (bf16[4,208,384]{2,1,0:T(8,128)(2,1)S(1)}, bf16[4,208,384]{2,1,0:T(8,128)(2,1)}, u32[]{:S(2)}, u32[]{:S(2)}) collective-permute-start(bf16[4,208,384]{2,1,0:T(8,128)(2,1)S(1)} %broadcast_select_fusion.2), channel_id=1, source_target_pairs={{0,4},{1,5},{2,6},{3,7},{4,0},{5,1},{6,2},{7,3},{8,12},{9,13},{10,... | collective-permute-start | bytes 1916936 | tf_op jit(solution)/shard_map/ppermute | solution.py:723
  313.7 56.1 %collective-permute-start.13 = (bf16[192,3072]{1,0:T(8,128)(2,1)S(1)}, bf16[192,3072]{1,0:T(8,128)(2,1)S(1)}, u32[]{:S(2)}, u32[]{:S(2)}) collective-permute-start(bf16[192,3072]{1,0:T(8,128)(2,1)S(1)} %bitcast_add_fusion.6), channel_id=1, source_target_pairs={{0,8},{8,16},{1,9},{9,17},{2,10},{10,18},{3,11},{11,19},{4,12},{12... | collective-permute-start | bytes 3538952 | tf_op jit(solution)/shard_map/ppermute | solution.py:702
  321.9 48.0 %slice-start.2 = ((s8[4718592]{0:T(1024)(128)(4,1)}), s8[4194304]{0:T(1024)(128)(4,1)S(1)}, s32[]{:S(2)}) async-start(s8[4718592]{0:T(1024)(128)(4,1)} %bitcast.72), calls=%async_computation.6 | async-start | bytes 8388608
  323.6 46.2 %slice-start.3 = ((s8[4718592]{0:T(1024)(128)(4,1)}), s8[524288]{0:T(1024)(128)(4,1)S(1)}, s32[]{:S(2)}) async-start(s8[4718592]{0:T(1024)(128)(4,1)} %bitcast.72), calls=%async_computation.7 | async-start | bytes 1048576
  323.6 41.7 %collective-permute-start.3 = (bf16[208,384]{1,0:T(8,128)(2,1)S(1)}, bf16[208,384]{1,0:T(8,128)(2,1)S(1)}, u32[]{:S(2)}, u32[]{:S(2)}) collective-permute-start(bf16[208,384]{1,0:T(8,128)(2,1)S(1)} %get-tuple-element.72), channel_id=1, source_target_pairs={{0,8},{1,9},{2,10},{3,11},{4,12},{5,13},{6,14},{7,15}} | collective-permute-start | bytes 479240 | tf_op jit(solution)/shard_map/ppermute | solution.py:702
  341.2 66.7 %collective-permute-start.22 = (bf16[768,768]{1,0:T(8,128)(2,1)}, bf16[768,768]{1,0:T(8,128)(2,1)}, u32[]{:S(2)}, u32[]{:S(2)}) collective-permute-start(bf16[768,768]{1,0:T(8,128)(2,1)} %get-tuple-element.55), channel_id=1, source_target_pairs={{24,16},{16,8},{25,17},{17,9},{26,18},{18,10},{27,19},{19,11},{28,... | collective-permute-start | bytes 3538952 | tf_op jit(solution)/shard_map/ppermute | solution.py:705
  342.9 31.6 %collective-permute-start.6 = (bf16[208,384]{1,0:T(8,128)(2,1)S(1)}, bf16[208,384]{1,0:T(8,128)(2,1)S(1)}, u32[]{:S(2)}, u32[]{:S(2)}) collective-permute-start(bf16[208,384]{1,0:T(8,128)(2,1)S(1)} %get-tuple-element.73), channel_id=1, source_target_pairs={{24,16},{25,17},{26,18},{27,19},{28,20},{29,21},{30,22},{31,23}} | collective-permute-start | bytes 479240 | tf_op jit(solution)/shard_map/ppermute | solution.py:705
  365.4 9.0 %collective-permute-start.4 = (bf16[208,384]{1,0:T(8,128)(2,1)S(1)}, bf16[208,384]{1,0:T(8,128)(2,1)S(1)}, u32[]{:S(2)}, u32[]{:S(2)}) collective-permute-start(bf16[208,384]{1,0:T(8,128)(2,1)S(1)} %bitcast_add_fusion.10), channel_id=1, source_target_pairs={{0,8},{8,16},{1,9},{9,17},{2,10},{10,18},{3,11},{11,19},{4,12},{12... | collective-permute-start | bytes 479240 | tf_op jit(solution)/shard_map/ppermute | solution.py:702
  372.8 60.8 %collective-permute-start.16 = (bf16[192,3072]{1,0:T(8,128)(2,1)}, bf16[192,3072]{1,0:T(8,128)(2,1)}, u32[]{:S(2)}, u32[]{:S(2)}) collective-permute-start(bf16[192,3072]{1,0:T(8,128)(2,1)} %get-tuple-element.59), channel_id=1, source_target_pairs={{24,16},{16,8},{25,17},{17,9},{26,18},{18,10},{27,19},{19,11},{28,... | collective-permute-start | bytes 3538952 | tf_op jit(solution)/shard_map/ppermute | solution.py:705
  374.5 9.0 %collective-permute-start.7 = (bf16[208,384]{1,0:T(8,128)(2,1)S(1)}, bf16[208,384]{1,0:T(8,128)(2,1)S(1)}, u32[]{:S(2)}, u32[]{:S(2)}) collective-permute-start(bf16[208,384]{1,0:T(8,128)(2,1)S(1)} %get-tuple-element.71), channel_id=1, source_target_pairs={{24,16},{16,8},{25,17},{17,9},{26,18},{18,10},{27,19},{19,11},{28,... | collective-permute-start | bytes 479240 | tf_op jit(solution)/shard_map/ppermute | solution.py:705
  375.2 73.5 %collective-permute-start.20 = (bf16[768,768]{1,0:T(8,128)(2,1)}, bf16[768,768]{1,0:T(8,128)(2,1)S(1)}, u32[]{:S(2)}, u32[]{:S(2)}) collective-permute-start(bf16[768,768]{1,0:T(8,128)(2,1)} %get-tuple-element.54), channel_id=1, source_target_pairs={{0,8},{8,16},{16,24},{1,9},{9,17},{17,25},{2,10},{10,18},{18,26},{... | collective-permute-start | bytes 3538952 | tf_op jit(solution)/shard_map/ppermute | solution.py:702
  378.9 88.4 %collective-permute-start.14 = (bf16[192,3072]{1,0:T(8,128)(2,1)}, bf16[192,3072]{1,0:T(8,128)(2,1)S(1)}, u32[]{:S(2)}, u32[]{:S(2)}) collective-permute-start(bf16[192,3072]{1,0:T(8,128)(2,1)} %get-tuple-element.58), channel_id=1, source_target_pairs={{0,8},{8,16},{16,24},{1,9},{9,17},{17,25},{2,10},{10,18},{18,26},{... | collective-permute-start | bytes 3538952 | tf_op jit(solution)/shard_map/ppermute | solution.py:702
  383.5 48.6 %collective-permute-start.5 = (bf16[208,384]{1,0:T(8,128)(2,1)S(1)}, bf16[208,384]{1,0:T(8,128)(2,1)S(1)}, u32[]{:S(2)}, u32[]{:S(2)}) collective-permute-start(bf16[208,384]{1,0:T(8,128)(2,1)S(1)} %get-tuple-element.70), channel_id=1, source_target_pairs={{0,8},{8,16},{16,24},{1,9},{9,17},{17,25},{2,10},{10,18},{18,26},{... | collective-permute-start | bytes 479240 | tf_op jit(solution)/shard_map/ppermute | solution.py:702
  407.9 25.4 %collective-permute-start.8 = (bf16[208,384]{1,0:T(8,128)(2,1)S(1)}, bf16[208,384]{1,0:T(8,128)(2,1)S(1)}, u32[]{:S(2)}, u32[]{:S(2)}) collective-permute-start(bf16[208,384]{1,0:T(8,128)(2,1)S(1)} %bitcast_add_fusion.9), channel_id=1, source_target_pairs={{24,16},{16,8},{8,0},{25,17},{17,9},{9,1},{26,18},{18,10},{10,2},{... | collective-permute-start | bytes 479240 | tf_op jit(solution)/shard_map/ppermute | solution.py:705
  432.1 31.6 %collective-permute-start.23 = (bf16[768,768]{1,0:T(8,128)(2,1)}, bf16[768,768]{1,0:T(8,128)(2,1)}, u32[]{:S(2)}, u32[]{:S(2)}) collective-permute-start(bf16[768,768]{1,0:T(8,128)(2,1)} %bitcast_add_fusion.1), channel_id=1, source_target_pairs={{24,16},{16,8},{8,0},{25,17},{17,9},{9,1},{26,18},{18,10},{10,2},{... | collective-permute-start | bytes 3538952 | tf_op jit(solution)/shard_map/ppermute | solution.py:705
  433.4 5.3 %collective-permute-start.9 = (bf16[208,384]{1,0:T(8,128)(2,1)S(1)}, bf16[208,384]{1,0:T(8,128)(2,1)S(1)}, u32[]{:S(2)}, u32[]{:S(2)}) collective-permute-start(bf16[208,384]{1,0:T(8,128)(2,1)S(1)} %fusion.5), channel_id=1, source_target_pairs={{0,4},{1,5},{2,6},{3,7},{4,0},{5,1},{6,2},{7,3},{8,12},{9,13},{10,... | collective-permute-start | bytes 479240 | tf_op jit(solution)/shard_map/ppermute | solution.py:729
  436.3 49.9 %collective-permute-start.17 = (bf16[192,3072]{1,0:T(8,128)(2,1)}, bf16[192,3072]{1,0:T(8,128)(2,1)}, u32[]{:S(2)}, u32[]{:S(2)}) collective-permute-start(bf16[192,3072]{1,0:T(8,128)(2,1)} %bitcast_add_fusion.5), channel_id=1, source_target_pairs={{24,16},{16,8},{8,0},{25,17},{17,9},{9,1},{26,18},{18,10},{10,2},{... | collective-permute-start | bytes 3538952 | tf_op jit(solution)/shard_map/ppermute | solution.py:705
  438.9 28.2 %collective-permute-start.10 = (bf16[416,384]{1,0:T(8,128)(2,1)S(1)}, bf16[416,384]{1,0:T(8,128)(2,1)S(1)}, u32[]{:S(2)}, u32[]{:S(2)}) collective-permute-start(bf16[416,384]{1,0:T(8,128)(2,1)S(1)} %pad_maximum_fusion.2), channel_id=1, source_target_pairs={{0,2},{1,3},{2,0},{3,1},{4,6},{5,7},{6,4},{7,5},{8,10},{9,11},{10,... | collective-permute-start | bytes 958472 | tf_op jit(solution)/shard_map/ppermute | solution.py:729
  467.2 22.5 %collective-permute-start.11 = (bf16[832,384]{1,0:T(8,128)(2,1)S(1)}, bf16[832,384]{1,0:T(8,128)(2,1)S(1)}, u32[]{:S(2)}, u32[]{:S(2)}) collective-permute-start(bf16[832,384]{1,0:T(8,128)(2,1)S(1)} %pad_maximum_fusion.1), channel_id=1, source_target_pairs={{0,1},{1,0},{2,3},{3,2},{4,5},{5,4},{6,7},{7,6},{8,9},{9,8},{10,11... | collective-permute-start | bytes 1916936 | tf_op jit(solution)/shard_map/ppermute | solution.py:729
